TPU v7x, 32 devices: a whole 2x2x4 slice. The times are simulated.
32 devices in a mesh: groups: 2 (over y), ctx: 4 (over z), exp: 4 (over x, core), rep: 1.
Axes of the slice: x: 2, y: 2, z: 4, core: 2. Of those that a mesh axis runs over, the one named last changes fastest.
Arguments:
- queries: bfloat16 [2, 256, 4096], P('groups', 'ctx', ('exp', 'rep')), parts along dimension 0, may hold values from -16.25 to 16.25
- pages: bfloat16 [2, 2304, 2, 512], P('groups', 'ctx', None, 'exp'), parts along dimension 0, may hold values from -5.2 to 5.2
- cached_lengths: int32 [2, 4], P('groups'), parts along dimension 0, may hold values from 128 to 512
- residual_in: bfloat16 [2, 256, 2048], P('groups', ('ctx', 'exp')), parts along dimension 0, may hold values from -2.390625 to 2.390625
- out_weight: bfloat16 [4096, 2048], P(('exp', 'rep')), may hold values from -0.09375 to 0.09375
- norm_gain: float32 [2048], replicated, may hold values from 0.1 to 1.9
- expert_ids: int32 [2, 256, 8], P('groups', ('ctx', 'exp')), parts along dimension 0, may hold values from 0 to 15, all different within a row; in each aligned block of 16 rows (0 to 15, 16 to 31, ..., all dimensions but the last counted through in order) at most 8 rows name the same one
- route_scores: float32 [2, 256, 8], P('groups', ('ctx', 'exp')), parts along dimension 0, may hold values from 0.05 to 1
- expert_input: bfloat16 [16, 2048, 2, 384], P(('ctx', 'exp'), None, None, 'rep'), may hold values from -0.125 to 0.125
- expert_output: bfloat16 [16, 384, 2048], P(('ctx', 'exp'), 'rep'), may hold values from -0.3125 to 0.3125
Outputs:
- context: bfloat16 [2, 256, 4096], P('groups', 'ctx', ('exp', 'rep')), parts along dimension 0
- layer_out: bfloat16 [2, 256, 2048], P('groups', ('ctx', 'exp', 'rep')), parts along dimension 0
There are 2 independent parts, one for each index of `groups`. A program takes and returns all parts, laid end to end along the dimension named above; an argument that names none is the same for every part. Nothing has to cross between parts.
Inputs may be any that keep to these rules, and one draw needn't show every extreme that they name: `expert_ids`: in every aligned block of 16 positions of one request, no expert is named by more than 8 of the block's rows, and in some blocks one expert by exactly 8; the 8 experts of a row differ.
All inputs are finite; a program needn't handle non-finite values.
Results may differ from a plain program's by a relative error of at most 0.015.
Values may be sent and summed in bfloat16 or wider, within the bound.
A program may use at most 128 MiB of HBM per device.

v0:
```python
import functools

import jax
import jax.numpy as jnp
from jax import lax
from jax.experimental import pallas as pl
from jax.experimental.pallas import tpu as pltpu
from jax.sharding import PartitionSpec as P

HEAD = 128


floor_value = -1e30
norm_epsilon = 1e-06


def normalize(hidden, norm_gain):
    widened = hidden.astype(jnp.float32)
    mean_square = jnp.mean(widened * widened, axis=-1, keepdims=True)
    return (widened * lax.rsqrt(mean_square + norm_epsilon) * norm_gain).astype(jnp.bfloat16)


def attend_piece(query_rows, page_rows, allowed):
    scaling = query_rows.shape[-1] ** (-0.5)
    scores = (
        jnp.einsum(
            "rqhe,rke->rqhk", query_rows, page_rows[:, :, 0], preferred_element_type=jnp.float32
        )
        * scaling
    )
    permitted = allowed[:, :, None, :]
    masked = jnp.where(permitted, scores, floor_value)
    peaks = jnp.max(masked, axis=-1)
    weights = jnp.where(permitted, jnp.exp(masked - peaks[..., None]), 0.0)
    totals = jnp.sum(weights, axis=-1)
    summed = jnp.einsum(
        "rqhk,rke->rqhe",
        weights.astype(jnp.bfloat16),
        page_rows[:, :, 1],
        preferred_element_type=jnp.float32,
    )
    return (peaks, totals, summed)


def merge_partials(earlier, later):
    peaks = jnp.maximum(earlier[0], later[0])
    later_scale = jnp.exp(later[0] - peaks)
    totals = later[1] * later_scale
    summed = later[2] * later_scale[..., None]
    return (peaks, totals, summed)


def rows_mask(row_index, lengths, query_positions, slab_size, fresh_block):
    page_size = slab_size + fresh_block
    page_number = row_index // page_size
    offset = row_index - page_number * page_size
    page_count = lengths.shape[1]
    picker = page_number[None, :] == jnp.arange(page_count, dtype=jnp.int32)[:, None]
    live_length = jnp.sum(jnp.where(picker[None], lengths[:, :, None], 0), axis=1)
    in_cache = (offset < slab_size)[None, :] & (offset[None, :] < live_length)
    fresh_position = page_number * fresh_block + offset - slab_size
    in_fresh = (offset >= slab_size)[None, :] & (
        fresh_position[None, :] <= query_positions[:, None]
    )
    return in_cache[:, None, :] | in_fresh[None, :, :]


def per_device(
    queries,
    pages,
    cached_lengths,
    residual_in,
    out_weight,
    norm_gain,
    expert_ids,
    route_scores,
    expert_input,
    expert_output,
):
    requests, fresh_block, query_width = queries.shape
    local_heads = query_width // HEAD
    core_place = lax.axis_index("rep")
    page_place = lax.axis_index("ctx")
    rep_count = lax.axis_size("rep")
    page_size = pages.shape[1]
    slab_size = page_size - fresh_block
    own_positions = page_place * fresh_block + jnp.arange(fresh_block, dtype=jnp.int32)
    query_rows = queries.reshape(requests, fresh_block, local_heads, HEAD)
    start_state = (
        jnp.full((requests, fresh_block, local_heads), floor_value, jnp.float32),
        jnp.zeros((requests, fresh_block, local_heads), jnp.float32),
        jnp.zeros((requests, fresh_block, local_heads, HEAD), jnp.float32),
    )
    page_piece = lax.all_gather(pages, "ctx", axis=1, tiled=True)
    row_index = jnp.arange(page_piece.shape[1], dtype=jnp.int32)
    allowed = rows_mask(row_index, cached_lengths, own_positions, slab_size, fresh_block)
    peaks, totals, summed = merge_partials(
        start_state, attend_piece(query_rows, page_piece, allowed)
    )
    context = (
        (summed / totals[..., None])
        .astype(jnp.bfloat16)
        .reshape(requests, fresh_block, query_width)
    )
    projected = jnp.dot(
        context.reshape(requests * fresh_block, query_width),
        out_weight,
        preferred_element_type=jnp.float32,
    ).reshape(requests, fresh_block, -1)
    token_block = residual_in.shape[1]
    share_size = token_block // rep_count
    own_share = lax.psum_scatter(
        projected.astype(jnp.bfloat16), ("exp", "rep"), scatter_dimension=1, tiled=True
    ).astype(jnp.float32)
    own_residual = lax.dynamic_slice_in_dim(residual_in, core_place * share_size, share_size, 1)
    own_hidden = (own_residual.astype(jnp.float32) + own_share).astype(jnp.bfloat16)
    normed = lax.all_gather(normalize(own_hidden, norm_gain), "rep", axis=1, tiled=True)
    top_count = expert_ids.shape[2]
    expert_count = lax.axis_size("ctx") * lax.axis_size("exp")
    most_rows = max(2, (token_block * top_count + expert_count - 1) // expert_count)
    capacity = requests * most_rows
    model_width = normed.shape[2]
    token_count = requests * token_block
    flat_ids = expert_ids.reshape(-1)
    row_count = flat_ids.shape[0]
    chosen = (flat_ids[:, None] == jnp.arange(expert_count, dtype=jnp.int32)[None, :]).astype(
        jnp.int32
    )
    earlier_rows = jnp.cumsum(chosen, axis=0) - chosen
    slot_rank = jnp.sum(earlier_rows * chosen, axis=1)
    slot_index = flat_ids * capacity + slot_rank
    slot_onehot = (
        slot_index[:, None] == jnp.arange(expert_count * capacity, dtype=jnp.int32)[None, :]
    ).astype(jnp.bfloat16)
    token_onehot = (
        (jnp.arange(row_count, dtype=jnp.int32) // top_count)[:, None]
        == jnp.arange(token_count, dtype=jnp.int32)[None, :]
    ).astype(jnp.bfloat16)
    placement = jnp.dot(slot_onehot.T, token_onehot, preferred_element_type=jnp.float32).astype(
        jnp.bfloat16
    )
    outgoing = jnp.dot(
        placement, normed.reshape(token_count, model_width), preferred_element_type=jnp.float32
    )
    outgoing = outgoing.astype(jnp.bfloat16).reshape(expert_count, capacity, model_width)
    scores_sum = jnp.sum(route_scores, axis=2, keepdims=True)
    combine = (route_scores / scores_sum).astype(jnp.bfloat16).reshape(-1)
    gathering = jnp.dot(
        (token_onehot * combine[:, None]).T, slot_onehot, preferred_element_type=jnp.float32
    ).astype(jnp.bfloat16)
    gate_up = expert_input[0]
    down_weight = expert_output[0]
    arrived_rows = lax.all_to_all(outgoing, ("ctx", "exp"), split_axis=0, concat_axis=0, tiled=True)
    inner_rows = jnp.einsum(
        "nd,dgh->ngh",
        arrived_rows.reshape(-1, model_width),
        gate_up,
        preferred_element_type=jnp.float32,
    )
    activated = (jax.nn.silu(inner_rows[:, 0]) * inner_rows[:, 1]).astype(jnp.bfloat16)
    result = jnp.dot(activated, down_weight, preferred_element_type=jnp.float32).astype(
        jnp.bfloat16
    )
    returned = lax.all_to_all(
        result.reshape(arrived_rows.shape), ("ctx", "exp"), split_axis=0, concat_axis=0, tiled=True
    )
    mixture = jnp.dot(
        gathering,
        returned.reshape(expert_count * capacity, model_width),
        preferred_element_type=jnp.float32,
    )
    own_mixture = lax.psum_scatter(
        mixture.reshape(requests, token_block, model_width).astype(jnp.bfloat16),
        "rep",
        scatter_dimension=1,
        tiled=True,
    ).astype(jnp.float32)
    layer_out = (own_hidden.astype(jnp.float32) + own_mixture).astype(jnp.bfloat16)
    return (context, layer_out)


BF = jnp.bfloat16
F32 = jnp.float32
MESH = pl.DeviceIdType.MESH
VMEM_LIMIT = 60 * 1024 * 1024


def fused_kernel(
    ctx_count, exp_count, capacity,
    lengths, query, page, residual, gain, ids, scores, w_out, w_in, w_down,
    context_out, layer_out,
    kv, raw, q_rows, bias, peak, total, accum, wo, wi, wg, wu, wd,
    ids_all, scores_all, combine_all, place, gather,
    rs_full, rs_send, rs_recv, hidden, nz, x_send, x_recv, x_rows, y_send, y_recv, mix_send, mix_recv,
    kv_left, kv_right, kv_recv, w_sem,
    ids_s, ids_r, sc_s, sc_r, rs_s, rs_r, nz_s, nz_r, dx_s, dx_r, ret_s, ret_r, mix_s, mix_r,
):
    ci = lax.axis_index("ctx")
    ei = lax.axis_index("exp")
    fresh = query.shape[0]
    heads = query.shape[1] // HEAD
    page_size = page.shape[0]
    slab = page_size - fresh
    rows = residual.shape[0]
    width = residual.shape[1]
    top = ids.shape[0]
    chunks = kv.shape[1]
    chunk = kv.shape[2]
    scaling = HEAD ** (-0.5) * 1.4426950408889634

    def ctx_peer(k):
        return {"ctx": lax.rem(ci + k, ctx_count)}

    def exp_peer(k):
        return {"exp": lax.rem(ei + k, exp_count)}

    def remote(src, dst, ss, rs, where):
        return pltpu.make_async_remote_copy(
            src_ref=src, dst_ref=dst, send_sem=ss, recv_sem=rs, device_id=where, device_id_type=MESH
        )

    copies_w = [
        pltpu.make_async_copy(w_out, wo, w_sem.at[0]),
        pltpu.make_async_copy(w_in, wi, w_sem.at[1]),
        pltpu.make_async_copy(w_down, wd, w_sem.at[2]),
    ]

    own_page = [
        pltpu.make_async_copy(page.at[pl.ds(c * chunk, chunk)], raw.at[c], kv_recv.at[ci, c])
        for c in range(chunks)
    ]
    for c in own_page:
        c.start()

    barrier = pltpu.get_barrier_semaphore()
    for k in range(1, ctx_count):
        pl.semaphore_signal(barrier, inc=1, device_id=ctx_peer(k), device_id_type=MESH)
    for k in range(1, exp_count):
        pl.semaphore_signal(barrier, inc=1, device_id=exp_peer(k), device_id_type=MESH)
    for c in range(chunks):
        own_page[c].wait()
        both = raw[c]
        kv[ci, c, :, :HEAD] = both[:, 0, :]
        kv[ci, c, :, HEAD:] = both[:, 1, :]
    pl.semaphore_wait(barrier, ctx_count + exp_count - 2)

    def right_copy(p, c):
        return remote(kv.at[p, c], kv.at[p, c], kv_right.at[p, c], kv_recv.at[p, c], {"ctx": ci + 1})

    def left_copy(p, c):
        return remote(kv.at[p, c], kv.at[p, c], kv_left.at[p, c], kv_recv.at[p, c], {"ctx": ci - 1})

    for c in range(chunks):
        @pl.when(ci < ctx_count - 1)
        def _():
            right_copy(ci, c).start()

        @pl.when(ci > 0)
        def _():
            left_copy(ci, c).start()

    small = []
    for k in range(1, ctx_count):
        small.append(remote(ids, ids_all.at[k], ids_s.at[k], ids_r.at[k], ctx_peer(k)))
        small.append(remote(scores, scores_all.at[k], sc_s.at[k], sc_r.at[k], ctx_peer(k)))
    for c in small:
        c.start()
    for c in copies_w:
        c.start()

    for h in range(heads):
        q_rows[h * fresh:(h + 1) * fresh, :] = query[:, h * HEAD:(h + 1) * HEAD]
    accum[...] = jnp.zeros_like(accum)
    total[...] = jnp.zeros_like(total)
    peak[...] = jnp.full_like(peak, floor_value)

    step_rows = lax.broadcasted_iota(jnp.int32, (fresh, chunk), 1)
    position = lax.broadcasted_iota(jnp.int32, (fresh, chunk), 0) + ci * fresh

    def mask(p, c):
        offset = step_rows + c * chunk
        cached = (offset < slab) & (offset < lengths[p])
        new = (offset >= slab) & (p * fresh + offset - slab <= position)
        bias[...] = jnp.where(cached | new, 0.0, floor_value)

    def attend(source):
        keys = source[:, :HEAD]
        values = source[:, HEAD:]
        step = 2 if heads % 2 == 0 else 1
        for h in range(0, heads, step):
            sl = slice(h * fresh, (h + step) * fresh)
            s = lax.dot_general(
                q_rows[sl, :], keys, (((1,), (1,)), ((), ())), preferred_element_type=F32
            )
            s = jnp.concatenate([s[i * fresh:(i + 1) * fresh] + bias[...] for i in range(step)], 0)
            old = peak[sl, :]
            now = jnp.maximum(old, jnp.max(s, axis=1, keepdims=True))
            w = jnp.exp2((s - now[:, :1]) * scaling)
            fade = jnp.exp2((old - now) * scaling)
            total[sl, :] = total[sl, :] * fade + jnp.sum(w, axis=1, keepdims=True)
            accum[sl, :] = accum[sl, :] * fade + jnp.dot(
                w.astype(BF), values, preferred_element_type=F32
            )
            peak[sl, :] = now

    def own_chunk(c, carry):
        mask(ci, c)
        attend(kv.at[ci, c])
        return carry

    lax.fori_loop(0, chunks, own_chunk, 0)

    copies_w[1].wait()
    depth = 256

    def unpack(i, carry):
        at = pl.ds(pl.multiple_of(i * depth, depth), depth)
        block = wi[at]
        wg[at, :] = block[:, 0, :]
        wu[at, :] = block[:, 1, :]
        return carry

    lax.fori_loop(0, width // depth, unpack, 0)

    combined = scores[...] / jnp.sum(scores[...], axis=0, keepdims=True)
    ids_all[0] = ids[...]
    combine_all[0] = combined.astype(BF).astype(F32)
    for c in small:
        c.wait()
    for k in range(1, ctx_count):
        given = scores_all[k]
        combine_all[k] = (given / jnp.sum(given, axis=0, keepdims=True)).astype(BF).astype(F32)

    lanes = exp_count * capacity
    lane = lax.broadcasted_iota(jnp.int32, (lanes, rows), 0)
    wanted = ci * exp_count + lax.rem(ei + lane // capacity, exp_count)
    seat = (lane - lane // capacity * capacity).astype(F32)
    earlier = (
        lax.broadcasted_iota(jnp.int32, (rows, rows), 0)
        < lax.broadcasted_iota(jnp.int32, (rows, rows), 1)
    ).astype(F32)
    for k in range(ctx_count):
        chosen = jnp.zeros((lanes, rows), F32)
        portion = jnp.zeros((lanes, rows), F32)
        for j in range(top):
            hit = ids_all[k, j:j + 1, :] == wanted
            chosen = jnp.where(hit, 1.0, chosen)
            portion = jnp.where(hit, combine_all[k, j:j + 1, :], portion)
        rank = jnp.dot(chosen.astype(BF), earlier.astype(BF), preferred_element_type=F32)
        seated = (chosen > 0.5) & (rank == seat)
        place[k] = jnp.where(seated, 1.0, 0.0)
        gather[k] = jnp.where(seated, portion, 0.0)

    def arrival(i, carry):
        d = i // (2 * chunks) + 1
        c = lax.rem(i // 2, chunks)
        p = jnp.where(lax.rem(i, 2) == 0, ci - d, ci + d)

        @pl.when((p >= 0) & (p < ctx_count))
        def _():
            mask(p, c)
            right_copy(p, c).wait_recv()

            @pl.when((p < ci) & (ci < ctx_count - 1))
            def _():
                right_copy(p, c).start()

            @pl.when((p > ci) & (ci > 0))
            def _():
                left_copy(p, c).start()

            attend(kv.at[p, c])

        return carry

    lax.fori_loop(0, 2 * (ctx_count - 1) * chunks, arrival, 0)

    for h in range(heads):
        sl = slice(h * fresh, (h + 1) * fresh)
        context_out[:, h * HEAD:(h + 1) * HEAD] = (accum[sl, :] / total[sl, :]).astype(BF)

    copies_w[0].wait()

    pieces = 4
    piece = width // pieces
    own_share = []
    rs_copies = []
    for n in range(pieces):
        cols = slice(n * piece, (n + 1) * piece)
        part = jnp.dot(context_out[...], wo[:, cols], preferred_element_type=F32)
        rs_full[n] = part
        for k in range(1, exp_count):
            at = pl.ds(pl.multiple_of(lax.rem(ei + k, exp_count) * rows, rows), rows)
            rs_send[k, n] = rs_full[n, at, :].astype(BF)
            c = remote(rs_send.at[k, n], rs_recv.at[k, n], rs_s.at[k, n], rs_r.at[k, n], exp_peer(k))
            c.start()
            rs_copies.append(c)
    mine = pl.ds(pl.multiple_of(ei * rows, rows), rows)
    square = jnp.zeros((rows, 1), F32)
    for n in range(pieces):
        cols = slice(n * piece, (n + 1) * piece)
        share = rs_full[n, mine, :]
        for k in range(1, exp_count):
            rs_copies[n * (exp_count - 1) + k - 1].wait_recv()
            share = share + rs_recv[k, n].astype(F32)
        h = (residual[:, cols].astype(F32) + share).astype(BF)
        hidden[:, cols] = h
        wide = h.astype(F32)
        square = square + jnp.sum(wide * wide, axis=1, keepdims=True)
    inverse = lax.rsqrt(square / width + norm_epsilon)
    nz[0] = (hidden[...].astype(F32) * inverse * gain[...]).astype(BF)

    nz_copies = {}
    order = [1, ctx_count - 1] + list(range(2, ctx_count - 1)) if ctx_count > 2 else list(range(1, ctx_count))
    for k in reversed(order):
        c = remote(nz.at[0], nz.at[k], nz_s.at[k], nz_r.at[k], ctx_peer(k))
        c.start()
        nz_copies[k] = c

    dx_copies = []
    ret_copies = []
    mix_copies = {}
    own = None
    places = [0] + order
    stages = [places]

    def dispatch(k):
        if k:
            nz_copies[k].wait_recv()
        routed = jnp.dot(place[k].astype(BF), nz[k], preferred_element_type=F32)
        for j in range(exp_count):
            block = routed[j * capacity:(j + 1) * capacity].astype(BF)
            if j == 0:
                x_recv[0, k] = block
            else:
                x_send[j, k] = block
                c = remote(x_send.at[j, k], x_recv.at[j, k], dx_s.at[j, k], dx_r.at[j, k], exp_peer(j))
                c.start()
                dx_copies.append(c)

    def experts(group):
        for k in group:
            for j in range(1, exp_count):
                dx_copies[places.index(k) * (exp_count - 1) + j - 1].wait_recv()
        count = len(group) * exp_count * capacity
        for j in range(exp_count):
            for n, k in enumerate(group):
                at = slice((j * len(group) + n) * capacity, (j * len(group) + n + 1) * capacity)
                x_rows[at, :] = x_recv[j, k].astype(F32)
        x = x_rows[:count, :].astype(BF)
        gate = jnp.dot(x, wg[...], preferred_element_type=F32)
        up = jnp.dot(x, wu[...], preferred_element_type=F32)
        act = (gate / (1.0 + jnp.exp(-gate)) * up).astype(BF)
        result = jnp.dot(act, wd[...], preferred_element_type=F32)
        for n, k in enumerate(group):
            for j in range(exp_count):
                first = (j * len(group) + n) * capacity
                block = result[first:first + capacity].astype(BF)
                if j == 0:
                    y_recv[0, k] = block
                else:
                    y_send[j, k] = block
                    c = remote(y_send.at[j, k], y_recv.at[j, k], ret_s.at[j, k], ret_r.at[j, k], exp_peer(exp_count - j))
                    c.start()
                    ret_copies.append(c)

    def mixing(k):
        for j in range(1, exp_count):
            ret_copies[places.index(k) * (exp_count - 1) + j - 1].wait_recv()
        rows_k = jnp.concatenate([y_recv[j, k].astype(F32) for j in range(exp_count)], 0).astype(BF)
        mixed = lax.dot_general(
            gather[k].astype(BF), rows_k, (((0,), (0,)), ((), ())), preferred_element_type=F32
        )
        if k == 0:
            return mixed
        mix_send[k] = mixed.astype(BF)
        c = remote(mix_send.at[k], mix_recv.at[k], mix_s.at[k], mix_r.at[k], ctx_peer(ctx_count - k))
        c.start()
        mix_copies[k] = c

    for k in stages[0]:
        dispatch(k)
    copies_w[2].wait()
    experts(stages[0])
    for group in stages[1:]:
        for k in group:
            dispatch(k)
        experts(group)
    for k in places[1:]:
        mixing(k)
    own = mixing(0)
    out = hidden[...].astype(F32) + own
    for k in order:
        mix_copies[k].wait_recv()
        out = out + mix_recv[k].astype(F32)
    layer_out[...] = out.astype(BF)

    for c in rs_copies + list(nz_copies.values()) + dx_copies + ret_copies + list(mix_copies.values()):
        c.wait_send()

    for c in range(chunks):
        @pl.when(ci < ctx_count - 1)
        def _():
            right_copy(ci, c).wait_send()

        @pl.when(ci > 0)
        def _():
            left_copy(ci, c).wait_send()

    def drain(i, carry):
        p = i // chunks
        c = lax.rem(i, chunks)

        @pl.when((p < ci) & (ci < ctx_count - 1))
        def _():
            right_copy(p, c).wait_send()

        @pl.when((p > ci) & (ci > 0))
        def _():
            left_copy(p, c).wait_send()

        return carry

    lax.fori_loop(0, ctx_count * chunks, drain, 0)


def settle(context, layer, context_out, layer_out):
    context_out[...] = context[...]
    layer_out[...] = layer[...]


def fused_device(
    ctx_count, exp_count, queries, pages, cached_lengths, residual_in, out_weight, norm_gain,
    expert_ids, route_scores, expert_input, expert_output,
):
    fresh, query_width = queries.shape[1:]
    page_size = pages.shape[1]
    rows, width = residual_in.shape[1:]
    top = expert_ids.shape[2]
    hidden_width = expert_input.shape[3]
    experts = ctx_count * exp_count
    capacity = max(2, -(-rows * top // experts))
    stacked = query_width // HEAD * fresh
    span = ctx_count * capacity
    vm = pl.BlockSpec(memory_space=pltpu.VMEM)
    sm = pl.BlockSpec(memory_space=pltpu.SMEM)
    hbm = pl.BlockSpec(memory_space=pl.ANY)
    dma = pltpu.SemaphoreType.DMA
    V = pltpu.VMEM
    lanes = exp_count * capacity
    pieces = 4
    chunks = next(n for n in (3, 2, 1) if page_size % (16 * n) == 0 or n == 1)
    context, layer_out = pl.pallas_call(
        functools.partial(fused_kernel, ctx_count, exp_count, capacity),
        out_shape=(
            jax.ShapeDtypeStruct((fresh, query_width), BF),
            jax.ShapeDtypeStruct((rows, width), BF),
        ),
        in_specs=[sm, vm, hbm, vm, vm, vm, vm, hbm, hbm, hbm],
        out_specs=(vm, vm),
        scratch_shapes=[
            V((ctx_count, chunks, page_size // chunks, 2 * HEAD), BF),
            V((chunks, page_size // chunks) + pages.shape[2:], BF),
            V((stacked, HEAD), BF),
            V((fresh, page_size // chunks), F32),
            V((stacked, HEAD), F32),
            V((stacked, HEAD), F32),
            V((stacked, HEAD), F32),
            V(out_weight.shape, BF),
            V(expert_input.shape[1:], BF),
            V((width, hidden_width), BF),
            V((width, hidden_width), BF),
            V(expert_output.shape[1:], BF),
            V((ctx_count, top, rows), jnp.int32),
            V((ctx_count, top, rows), F32),
            V((ctx_count, top, rows), F32),
            V((ctx_count, lanes, rows), F32),
            V((ctx_count, lanes, rows), F32),
            V((pieces, fresh, width // pieces), F32),
            V((exp_count, pieces, rows, width // pieces), BF),
            V((exp_count, pieces, rows, width // pieces), BF),
            V((rows, width), BF),
            V((ctx_count, rows, width), BF),
            V((exp_count, ctx_count, capacity, width), BF),
            V((exp_count, ctx_count, capacity, width), BF),
            V((exp_count * span, width), F32),
            V((exp_count, ctx_count, capacity, width), BF),
            V((exp_count, ctx_count, capacity, width), BF),
            V((ctx_count, rows, width), BF),
            V((ctx_count, rows, width), BF),
            dma((ctx_count, chunks)), dma((ctx_count, chunks)), dma((ctx_count, chunks)), dma((3,)),
            dma((ctx_count,)), dma((ctx_count,)), dma((ctx_count,)), dma((ctx_count,)),
            dma((exp_count, pieces)), dma((exp_count, pieces)),
            dma((ctx_count,)), dma((ctx_count,)),
            dma((exp_count, ctx_count)), dma((exp_count, ctx_count)),
            dma((exp_count, ctx_count)), dma((exp_count, ctx_count)),
            dma((ctx_count,)), dma((ctx_count,)),
        ],
        compiler_params=pltpu.CompilerParams(
            collective_id=0, has_side_effects=True, vmem_limit_bytes=VMEM_LIMIT
        ),
    )(
        cached_lengths[0], queries[0], pages[0], residual_in[0], norm_gain.reshape(1, width),
        expert_ids[0].T, route_scores[0].T, out_weight, expert_input[0], expert_output[0],
    )
    context, layer_out = pl.pallas_call(
        settle,
        out_shape=(
            jax.ShapeDtypeStruct(context.shape, BF),
            jax.ShapeDtypeStruct(layer_out.shape, BF),
        ),
        in_specs=[vm, vm],
        out_specs=(vm, vm),
    )(context, layer_out)
    return context[None], layer_out[None]


def fused_fits(mesh):
    return mesh.shape["rep"] == 1 and mesh.shape["ctx"] <= 8


def solution(mesh):
    in_specs = (
        P("groups", "ctx", ("exp", "rep")),
        P("groups", "ctx", None, "exp"),
        P("groups", None),
        P("groups", ("ctx", "exp"), None),
        P(("exp", "rep"), None),
        P(),
        P("groups", ("ctx", "exp"), None),
        P("groups", ("ctx", "exp"), None),
        P(("ctx", "exp"), None, None, "rep"),
        P(("ctx", "exp"), "rep", None),
    )
    out_specs = (P("groups", "ctx", ("exp", "rep")), P("groups", ("ctx", "exp", "rep"), None))
    body = per_device
    if fused_fits(mesh):
        body = functools.partial(fused_device, mesh.shape["ctx"], mesh.shape["exp"])
    return jax.shard_map(
        body, mesh=mesh, in_specs=in_specs, out_specs=out_specs, check_vma=False
    )
```

profile of v0, /device:TPU:0, one launch (start us, length us, event | category | flops | bytes accessed | tf_op | source)
XLA Modules:
  0.0 67.3 jit_solution(8062299655796407850)
XLA Ops:
  0.6 65.1 %shard_map.113 = (bf16[64,1024]{1,0:T(8,128)(2,1)}, bf16[16,2048]{1,0:T(8,128)(2,1)}) custom-call(s32[4]{0:T(128)} %bitcast.23, bf16[64,1024]{1,0:T(8,128)(2,1)} %bitcast.18, bf16[576,2,128]{2,1,0:T(2,128)(2,1)} %bitcast.17, bf16[16,2048]{1,0:T(8,128)(2,1)} %bitcast.19, f32[1,2048]{1,0:T(1,128)} %bitcast.20, s32[8,16]{1,0:T(8,128)} %bitcast.21, ...), custom_call_target="tpu_custom_call" | custom-call | tf_op jit(solution)/shard_map/pallas_call | solution.py:553
  65.7 1.6 %shard_map.114 = (bf16[64,1024]{1,0:T(8,128)(2,1)}, bf16[16,2048]{1,0:T(8,128)(2,1)}) custom-call(bf16[64,1024]{1,0:T(8,128)(2,1)} %get-tuple-element.6.context, bf16[16,2048]{1,0:T(8,128)(2,1)} %get-tuple-element.7.layer), custom_call_target="tpu_custom_call" | custom-call | tf_op jit(solution)/shard_map/pallas_call | solution.py:606
where the time goes:
time: 67.5 us; the launch traced here: 67.3 us
  Pallas kernels  66.7 us (99%)
    pallas_call x1, Pallas kernels, fused_device(): pl.pallas_call(functools.partial(fused_kernel, ctx_count, exp_count, capa...  65.1 us
    pallas_call x1, Pallas kernels, fused_device(): pl.pallas_call(settle, out_shape=(jax.ShapeDtypeStruct(context.shape, BF)...  1.59 us

commit v1 on v0

--- a/solution.py
+++ b/solution.py
@@ -187,25 +187,25 @@
 
 def fused_kernel(
     ctx_count, exp_count, capacity,
-    lengths, query, page, residual, gain, ids, scores, w_out, w_in, w_down,
+    lengths, query, page, residual_in, gain_in, ids_in, scores_in, w_out, w_in, w_down,
     context_out, layer_out,
-    kv, raw, q_rows, bias, peak, total, accum, wo, wi, wg, wu, wd,
+    lens, q_in, residual, gain, ids, scores,
+    raw, raw_fresh, kv, kv_fresh, q_rows, peak, accum, wo, wi, wg, wu, wd,
     ids_all, scores_all, combine_all, place, gather,
-    rs_full, rs_send, rs_recv, hidden, nz, x_send, x_recv, x_rows, y_send, y_recv, mix_send, mix_recv,
-    kv_left, kv_right, kv_recv, w_sem,
+    rs_full, rs_send, rs_recv, hidden, nz, x_send, x_recv, y_send, y_recv, mix_send, mix_recv,
+    own_sem, in_sem, kv_left, kv_right, kv_recv, w_sem,
     ids_s, ids_r, sc_s, sc_r, rs_s, rs_r, nz_s, nz_r, dx_s, dx_r, ret_s, ret_r, mix_s, mix_r,
 ):
     ci = lax.axis_index("ctx")
     ei = lax.axis_index("exp")
-    fresh = query.shape[0]
-    heads = query.shape[1] // HEAD
-    page_size = page.shape[0]
-    slab = page_size - fresh
+    fresh = q_in.shape[0]
+    heads = q_in.shape[1] // HEAD
+    halves = raw.shape[1]
+    half_rows = raw.shape[2]
+    slab = halves * half_rows
     rows = residual.shape[0]
     width = residual.shape[1]
     top = ids.shape[0]
-    chunks = kv.shape[1]
-    chunk = kv.shape[2]
     scaling = HEAD ** (-0.5) * 1.4426950408889634
 
     def ctx_peer(k):
@@ -219,115 +219,150 @@
             src_ref=src, dst_ref=dst, send_sem=ss, recv_sem=rs, device_id=where, device_id_type=MESH
         )
 
+    barrier = pltpu.get_barrier_semaphore()
+    for k in range(1, ctx_count):
+        pl.semaphore_signal(barrier, inc=1, device_id=ctx_peer(k), device_id_type=MESH)
+    for k in range(1, exp_count):
+        pl.semaphore_signal(barrier, inc=1, device_id=exp_peer(k), device_id_type=MESH)
+
+    def page_piece(c):
+        return page.at[pl.ds(c * half_rows, half_rows)] if c < halves else page.at[pl.ds(slab, fresh)]
+
+    def raw_piece(p, c):
+        return raw.at[p, c] if c < halves else raw_fresh.at[p]
+
+    pieces_in_order = [halves] + list(range(halves))
+    own_page = [pltpu.make_async_copy(page_piece(c), raw_piece(ci, c), own_sem.at[c]) for c in range(halves + 1)]
+    for c in pieces_in_order:
+        own_page[c].start()
+    inputs = [
+        pltpu.make_async_copy(src, dst, in_sem.at[n])
+        for n, (src, dst) in enumerate(
+            [(lengths, lens), (query, q_in), (residual_in, residual), (gain_in, gain), (ids_in, ids), (scores_in, scores)]
+        )
+    ]
+    for c in inputs:
+        c.start()
     copies_w = [
         pltpu.make_async_copy(w_out, wo, w_sem.at[0]),
         pltpu.make_async_copy(w_in, wi, w_sem.at[1]),
         pltpu.make_async_copy(w_down, wd, w_sem.at[2]),
     ]
-
-    own_page = [
-        pltpu.make_async_copy(page.at[pl.ds(c * chunk, chunk)], raw.at[c], kv_recv.at[ci, c])
-        for c in range(chunks)
-    ]
-    for c in own_page:
+    for n in (1, 0, 2):
+        copies_w[n].start()
+
+    kv[:, :, 2 * HEAD:] = jnp.ones(kv.shape[:2] + (HEAD,), BF)
+    kv_fresh[:, :2 * HEAD] = jnp.zeros((kv_fresh.shape[0], 2 * HEAD), BF)
+    kv_fresh[:, 2 * HEAD:] = jnp.ones((kv_fresh.shape[0], HEAD), BF)
+    accum[...] = jnp.zeros_like(accum)
+    peak[...] = jnp.full_like(peak, floor_value)
+    pl.semaphore_wait(barrier, ctx_count + exp_count - 2)
+
+    def send_right(p, c, src):
+        dst = raw_piece(p, c) if isinstance(c, int) else raw.at[p, c]
+        return remote(src, dst, kv_right.at[p, c], kv_recv.at[p, c], {"ctx": ci + 1})
+
+    def send_left(p, c, src):
+        dst = raw_piece(p, c) if isinstance(c, int) else raw.at[p, c]
+        return remote(src, dst, kv_left.at[p, c], kv_recv.at[p, c], {"ctx": ci - 1})
+
+    small = []
+    for k in range(1, ctx_count):
+        small.append(remote(ids_in, ids_all.at[ci], ids_s.at[k], ids_r.at[ci], ctx_peer(k)))
+        small.append(remote(scores_in, scores_all.at[ci], sc_s.at[k], sc_r.at[ci], ctx_peer(k)))
+    for c in small:
         c.start()
 
-    barrier = pltpu.get_barrier_semaphore()
-    for k in range(1, ctx_count):
-        pl.semaphore_signal(barrier, inc=1, device_id=ctx_peer(k), device_id_type=MESH)
-    for k in range(1, exp_count):
-        pl.semaphore_signal(barrier, inc=1, device_id=exp_peer(k), device_id_type=MESH)
-    for c in range(chunks):
-        own_page[c].wait()
-        both = raw[c]
-        kv[ci, c, :, :HEAD] = both[:, 0, :]
-        kv[ci, c, :, HEAD:] = both[:, 1, :]
-    pl.semaphore_wait(barrier, ctx_count + exp_count - 2)
-
-    def right_copy(p, c):
-        return remote(kv.at[p, c], kv.at[p, c], kv_right.at[p, c], kv_recv.at[p, c], {"ctx": ci + 1})
-
-    def left_copy(p, c):
-        return remote(kv.at[p, c], kv.at[p, c], kv_left.at[p, c], kv_recv.at[p, c], {"ctx": ci - 1})
-
-    for c in range(chunks):
+    for c in pieces_in_order:
         @pl.when(ci < ctx_count - 1)
         def _():
-            right_copy(ci, c).start()
-
-        @pl.when(ci > 0)
-        def _():
-            left_copy(ci, c).start()
-
-    small = []
-    for k in range(1, ctx_count):
-        small.append(remote(ids, ids_all.at[k], ids_s.at[k], ids_r.at[k], ctx_peer(k)))
-        small.append(remote(scores, scores_all.at[k], sc_s.at[k], sc_r.at[k], ctx_peer(k)))
-    for c in small:
-        c.start()
-    for c in copies_w:
-        c.start()
-
+            send_right(ci, c, page_piece(c)).start()
+
+        if c < halves:
+            @pl.when(ci > 0)
+            def _():
+                send_left(ci, c, page_piece(c)).start()
+
+    inputs[0].wait()
+    inputs[1].wait()
     for h in range(heads):
-        q_rows[h * fresh:(h + 1) * fresh, :] = query[:, h * HEAD:(h + 1) * HEAD]
-    accum[...] = jnp.zeros_like(accum)
-    total[...] = jnp.zeros_like(total)
-    peak[...] = jnp.full_like(peak, floor_value)
-
-    step_rows = lax.broadcasted_iota(jnp.int32, (fresh, chunk), 1)
-    position = lax.broadcasted_iota(jnp.int32, (fresh, chunk), 0) + ci * fresh
-
-    def mask(p, c):
-        offset = step_rows + c * chunk
-        cached = (offset < slab) & (offset < lengths[p])
-        new = (offset >= slab) & (p * fresh + offset - slab <= position)
-        bias[...] = jnp.where(cached | new, 0.0, floor_value)
-
-    def attend(source):
+        q_rows[h * fresh:(h + 1) * fresh, :] = q_in[:, h * HEAD:(h + 1) * HEAD]
+
+    step = next(n for n in (4, 2, 1) if heads % n == 0)
+    page_number = lax.broadcasted_iota(jnp.int32, (1, ctx_count), 1)
+    slab_row = lax.broadcasted_iota(jnp.int32, (1, slab), 1).astype(F32)
+
+    def split(p, c):
+        both = pltpu.einshape("sgh->gsh", raw[p, c])
+        at = pl.ds(pl.multiple_of(c * half_rows, half_rows), half_rows)
+        kv[p, at, :HEAD] = both[0]
+        kv[p, at, HEAD:2 * HEAD] = both[1]
+
+    def split_fresh(p):
+        both = pltpu.einshape("sgh->gsh", raw_fresh[p])
+        at = pl.ds(pl.multiple_of(p * fresh, fresh), fresh)
+        kv_fresh[at, :HEAD] = both[0]
+        kv_fresh[at, HEAD:2 * HEAD] = both[1]
+
+    def attend(source, bias):
         keys = source[:, :HEAD]
         values = source[:, HEAD:]
-        step = 2 if heads % 2 == 0 else 1
+        count = keys.shape[0]
         for h in range(0, heads, step):
             sl = slice(h * fresh, (h + step) * fresh)
             s = lax.dot_general(
                 q_rows[sl, :], keys, (((1,), (1,)), ((), ())), preferred_element_type=F32
             )
-            s = jnp.concatenate([s[i * fresh:(i + 1) * fresh] + bias[...] for i in range(step)], 0)
+            s = (s.reshape(step, fresh, count) + bias[None]).reshape(step * fresh, count)
             old = peak[sl, :]
             now = jnp.maximum(old, jnp.max(s, axis=1, keepdims=True))
             w = jnp.exp2((s - now[:, :1]) * scaling)
             fade = jnp.exp2((old - now) * scaling)
-            total[sl, :] = total[sl, :] * fade + jnp.sum(w, axis=1, keepdims=True)
-            accum[sl, :] = accum[sl, :] * fade + jnp.dot(
+            accum[sl, :] = accum[sl, :] * jnp.concatenate([fade, fade], 1) + jnp.dot(
                 w.astype(BF), values, preferred_element_type=F32
             )
             peak[sl, :] = now
 
-    def own_chunk(c, carry):
-        mask(ci, c)
-        attend(kv.at[ci, c])
-        return carry
-
-    lax.fori_loop(0, chunks, own_chunk, 0)
-
+    def attend_page(p):
+        live = jnp.sum(jnp.where(page_number == p, lens[...], 0).astype(F32), axis=1, keepdims=True)
+        attend(kv.at[p], jnp.where(slab_row < live, 0.0, floor_value))
+
+    def attend_fresh():
+        count = kv_fresh.shape[0]
+        position = lax.broadcasted_iota(jnp.int32, (fresh, count), 0) + ci * fresh
+        attend(kv_fresh, jnp.where(lax.broadcasted_iota(jnp.int32, (fresh, count), 1) <= position, 0.0, floor_value))
+
+    own_page[halves].wait()
+    split_fresh(ci)
+    for c in range(halves):
+        own_page[c].wait()
+        split(ci, c)
+    attend_page(ci)
+
+    steps = 2 * halves * (ctx_count - 1)
+    depth = next(n for n in range(-(-width // (steps + 4)), width + 1) if width % n == 0 and n % 16 == 0)
+    blocks = width // depth
     copies_w[1].wait()
-    depth = 256
-
-    def unpack(i, carry):
+
+    def unpack(i):
         at = pl.ds(pl.multiple_of(i * depth, depth), depth)
-        block = wi[at]
-        wg[at, :] = block[:, 0, :]
-        wu[at, :] = block[:, 1, :]
-        return carry
-
-    lax.fori_loop(0, width // depth, unpack, 0)
-
-    combined = scores[...] / jnp.sum(scores[...], axis=0, keepdims=True)
-    ids_all[0] = ids[...]
-    combine_all[0] = combined.astype(BF).astype(F32)
-    for c in small:
+        block = pltpu.einshape("dgh->gdh", wi[at])
+        wg[at, :] = block[0]
+        wu[at, :] = block[1]
+
+    ahead = max(0, blocks - steps)
+    for i in range(ahead):
+        unpack(i)
+
+    for c in inputs[2:]:
         c.wait()
+    ids_all[ci] = ids[...]
+    scores_all[ci] = scores[...]
     for k in range(1, ctx_count):
+        source = lax.rem(ci + k, ctx_count)
+        remote(ids_in, ids_all.at[source], ids_s.at[k], ids_r.at[source], ctx_peer(k)).wait_recv()
+        remote(scores_in, scores_all.at[source], sc_s.at[k], sc_r.at[source], ctx_peer(k)).wait_recv()
+    for k in range(ctx_count):
         given = scores_all[k]
         combine_all[k] = (given / jnp.sum(given, axis=0, keepdims=True)).astype(BF).astype(F32)
 
@@ -351,33 +386,54 @@
         place[k] = jnp.where(seated, 1.0, 0.0)
         gather[k] = jnp.where(seated, portion, 0.0)
 
+    def pass_on(p, c):
+        src = raw_piece(p, c) if isinstance(c, int) else raw.at[p, c]
+
+        @pl.when((p < ci) & (ci < ctx_count - 1))
+        def _():
+            send_right(p, c, src).start()
+
+        if not (isinstance(c, int) and c == halves):
+            @pl.when((p > ci) & (ci > 0))
+            def _():
+                send_left(p, c, src).start()
+
     def arrival(i, carry):
-        d = i // (2 * chunks) + 1
-        c = lax.rem(i // 2, chunks)
+        d = i // (2 * halves) + 1
+        c = lax.rem(i // 2, halves)
         p = jnp.where(lax.rem(i, 2) == 0, ci - d, ci + d)
 
         @pl.when((p >= 0) & (p < ctx_count))
         def _():
-            mask(p, c)
-            right_copy(p, c).wait_recv()
-
-            @pl.when((p < ci) & (ci < ctx_count - 1))
+            @pl.when((c == 0) & (p < ci))
             def _():
-                right_copy(p, c).start()
-
-            @pl.when((p > ci) & (ci > 0))
+                send_right(p, halves, raw_fresh.at[p]).wait_recv()
+                pass_on(p, halves)
+                split_fresh(p)
+
+            send_right(p, c, raw.at[p, c]).wait_recv()
+            pass_on(p, c)
+            split(p, c)
+
+            @pl.when(c == halves - 1)
             def _():
-                left_copy(p, c).start()
-
-            attend(kv.at[p, c])
+                attend_page(p)
+
+        @pl.when(i == jnp.maximum(ci - 1, 0) * 2 * halves)
+        def _():
+            attend_fresh()
+
+        @pl.when(i + ahead < blocks)
+        def _():
+            unpack(i + ahead)
 
         return carry
 
-    lax.fori_loop(0, 2 * (ctx_count - 1) * chunks, arrival, 0)
+    lax.fori_loop(0, steps, arrival, 0)
 
     for h in range(heads):
         sl = slice(h * fresh, (h + 1) * fresh)
-        context_out[:, h * HEAD:(h + 1) * HEAD] = (accum[sl, :] / total[sl, :]).astype(BF)
+        context_out[:, h * HEAD:(h + 1) * HEAD] = (accum[sl, :HEAD] / accum[sl, HEAD:]).astype(BF)
 
     copies_w[0].wait()
 
@@ -408,125 +464,139 @@
         wide = h.astype(F32)
         square = square + jnp.sum(wide * wide, axis=1, keepdims=True)
     inverse = lax.rsqrt(square / width + norm_epsilon)
-    nz[0] = (hidden[...].astype(F32) * inverse * gain[...]).astype(BF)
-
-    nz_copies = {}
-    order = [1, ctx_count - 1] + list(range(2, ctx_count - 1)) if ctx_count > 2 else list(range(1, ctx_count))
-    for k in reversed(order):
-        c = remote(nz.at[0], nz.at[k], nz_s.at[k], nz_r.at[k], ctx_peer(k))
+    nz[ci] = (hidden[...].astype(F32) * inverse * gain[...]).astype(BF)
+
+    last = ctx_count - 1
+    middle = last / 2
+    send_table, work_table = [], []
+    for c in range(ctx_count):
+        others = [p for p in range(ctx_count) if p != c]
+        send_table.append(sorted(others, key=lambda p: (abs(p - c) % last, abs(p - middle))))
+        work_table.append([c] + sorted(others, key=lambda p: ((abs(p - c) - 1) % (last - 1) if last > 1 else 0, abs(p - middle))))
+
+    def lookup(table, n):
+        value = jnp.int32(table[0][n])
+        for c in range(1, ctx_count):
+            value = jnp.where(ci == c, table[c][n], value)
+        return value
+
+    def nz_copy(p, n, where):
+        return remote(nz.at[p], nz.at[p], nz_s.at[n], nz_r.at[p], {"ctx": where})
+
+    nz_copies = []
+    for n in range(last):
+        c = nz_copy(ci, n, lookup(send_table, n))
         c.start()
-        nz_copies[k] = c
-
-    dx_copies = []
-    ret_copies = []
-    mix_copies = {}
-    own = None
-    places = [0] + order
-    stages = [places]
-
-    def dispatch(k):
-        if k:
-            nz_copies[k].wait_recv()
-        routed = jnp.dot(place[k].astype(BF), nz[k], preferred_element_type=F32)
-        for j in range(exp_count):
+        nz_copies.append(c)
+
+    places = [lookup(work_table, n) for n in range(ctx_count)]
+
+    def dx_copy(j, n):
+        p = places[n]
+        return remote(x_send.at[j, p], x_recv.at[j, p], dx_s.at[j, p], dx_r.at[j, p], exp_peer(j))
+
+    def ret_copy(j, n):
+        p = places[n]
+        return remote(y_send.at[j, p], y_recv.at[j, p], ret_s.at[j, p], ret_r.at[j, p], exp_peer(exp_count - j))
+
+    def mix_copy(n):
+        p = places[n]
+        return remote(mix_send.at[p], mix_recv.at[ci], mix_s.at[p], mix_r.at[ci], {"ctx": p})
+
+    def dispatch(n):
+        p = places[n]
+        if n:
+            nz_copy(p, 0, p).wait_recv()
+        routed = jnp.dot(place[p].astype(BF), nz[p], preferred_element_type=F32)
+        for j in list(range(1, exp_count)) + [0]:
             block = routed[j * capacity:(j + 1) * capacity].astype(BF)
             if j == 0:
-                x_recv[0, k] = block
+                x_recv[0, p] = block
             else:
-                x_send[j, k] = block
-                c = remote(x_send.at[j, k], x_recv.at[j, k], dx_s.at[j, k], dx_r.at[j, k], exp_peer(j))
-                c.start()
-                dx_copies.append(c)
-
-    def experts(group):
-        for k in group:
-            for j in range(1, exp_count):
-                dx_copies[places.index(k) * (exp_count - 1) + j - 1].wait_recv()
-        count = len(group) * exp_count * capacity
-        for j in range(exp_count):
-            for n, k in enumerate(group):
-                at = slice((j * len(group) + n) * capacity, (j * len(group) + n + 1) * capacity)
-                x_rows[at, :] = x_recv[j, k].astype(F32)
-        x = x_rows[:count, :].astype(BF)
+                x_send[j, p] = block
+                dx_copy(j, n).start()
+
+    def experts(n):
+        p = places[n]
+        for j in range(1, exp_count):
+            dx_copy(j, n).wait_recv()
+        x = jnp.concatenate([x_recv[j, p].astype(F32) for j in range(exp_count)], 0).astype(BF)
         gate = jnp.dot(x, wg[...], preferred_element_type=F32)
         up = jnp.dot(x, wu[...], preferred_element_type=F32)
         act = (gate / (1.0 + jnp.exp(-gate)) * up).astype(BF)
         result = jnp.dot(act, wd[...], preferred_element_type=F32)
-        for n, k in enumerate(group):
-            for j in range(exp_count):
-                first = (j * len(group) + n) * capacity
-                block = result[first:first + capacity].astype(BF)
-                if j == 0:
-                    y_recv[0, k] = block
-                else:
-                    y_send[j, k] = block
-                    c = remote(y_send.at[j, k], y_recv.at[j, k], ret_s.at[j, k], ret_r.at[j, k], exp_peer(exp_count - j))
-                    c.start()
-                    ret_copies.append(c)
-
-    def mixing(k):
+        for j in list(range(1, exp_count)) + [0]:
+            block = result[j * capacity:(j + 1) * capacity].astype(BF)
+            if j == 0:
+                y_recv[0, p] = block
+            else:
+                y_send[j, p] = block
+                ret_copy(j, n).start()
+
+    def mixing(n):
+        p = places[n]
         for j in range(1, exp_count):
-            ret_copies[places.index(k) * (exp_count - 1) + j - 1].wait_recv()
-        rows_k = jnp.concatenate([y_recv[j, k].astype(F32) for j in range(exp_count)], 0).astype(BF)
+            ret_copy(j, n).wait_recv()
+        rows_p = jnp.concatenate([y_recv[j, p].astype(F32) for j in range(exp_count)], 0).astype(BF)
         mixed = lax.dot_general(
-            gather[k].astype(BF), rows_k, (((0,), (0,)), ((), ())), preferred_element_type=F32
+            gather[p].astype(BF), rows_p, (((0,), (0,)), ((), ())), preferred_element_type=F32
         )
-        if k == 0:
+        if n == 0:
             return mixed
-        mix_send[k] = mixed.astype(BF)
-        c = remote(mix_send.at[k], mix_recv.at[k], mix_s.at[k], mix_r.at[k], ctx_peer(ctx_count - k))
-        c.start()
-        mix_copies[k] = c
-
-    for k in stages[0]:
-        dispatch(k)
-    copies_w[2].wait()
-    experts(stages[0])
-    for group in stages[1:]:
-        for k in group:
-            dispatch(k)
-        experts(group)
-    for k in places[1:]:
-        mixing(k)
-    own = mixing(0)
-    out = hidden[...].astype(F32) + own
-    for k in order:
-        mix_copies[k].wait_recv()
-        out = out + mix_recv[k].astype(F32)
+        mix_send[p] = mixed.astype(BF)
+        mix_copy(n).start()
+
+    dispatch(0)
+    for n in range(1, ctx_count):
+        dispatch(n)
+        if n == 1:
+            copies_w[2].wait()
+        experts(n - 1)
+        if n > 2:
+            mixing(n - 2)
+    experts(ctx_count - 1)
+    for n in range(max(1, ctx_count - 2), ctx_count):
+        mixing(n)
+    out = hidden[...].astype(F32) + mixing(0)
+    for n in range(1, ctx_count):
+        p = places[n]
+        remote(mix_send.at[p], mix_recv.at[p], mix_s.at[p], mix_r.at[p], {"ctx": p}).wait_recv()
+        out = out + mix_recv[p].astype(F32)
     layer_out[...] = out.astype(BF)
 
-    for c in rs_copies + list(nz_copies.values()) + dx_copies + ret_copies + list(mix_copies.values()):
+    for c in rs_copies + nz_copies + small:
         c.wait_send()
-
-    for c in range(chunks):
+    for n in range(ctx_count):
+        for j in range(1, exp_count):
+            dx_copy(j, n).wait_send()
+            ret_copy(j, n).wait_send()
+        if n:
+            mix_copy(n).wait_send()
+
+    for c in pieces_in_order:
         @pl.when(ci < ctx_count - 1)
         def _():
-            right_copy(ci, c).wait_send()
-
-        @pl.when(ci > 0)
-        def _():
-            left_copy(ci, c).wait_send()
-
-    def drain(i, carry):
-        p = i // chunks
-        c = lax.rem(i, chunks)
-
-        @pl.when((p < ci) & (ci < ctx_count - 1))
-        def _():
-            right_copy(p, c).wait_send()
-
-        @pl.when((p > ci) & (ci > 0))
-        def _():
-            left_copy(p, c).wait_send()
+            send_right(ci, c, page_piece(c)).wait_send()
+
+        if c < halves:
+            @pl.when(ci > 0)
+            def _():
+                send_left(ci, c, page_piece(c)).wait_send()
+
+    def drain(p, carry):
+        for c in pieces_in_order:
+            @pl.when((p < ci) & (ci < ctx_count - 1))
+            def _():
+                send_right(p, c, raw_piece(p, c)).wait_send()
+
+            if c < halves:
+                @pl.when((p > ci) & (ci > 0))
+                def _():
+                    send_left(p, c, raw_piece(p, c)).wait_send()
 
         return carry
 
-    lax.fori_loop(0, ctx_count * chunks, drain, 0)
-
-
-def settle(context, layer, context_out, layer_out):
-    context_out[...] = context[...]
-    layer_out[...] = layer[...]
+    lax.fori_loop(0, ctx_count, drain, 0)
 
 
 def fused_device(
@@ -535,37 +605,39 @@
 ):
     fresh, query_width = queries.shape[1:]
     page_size = pages.shape[1]
+    slab = page_size - fresh
     rows, width = residual_in.shape[1:]
     top = expert_ids.shape[2]
     hidden_width = expert_input.shape[3]
     experts = ctx_count * exp_count
     capacity = max(2, -(-rows * top // experts))
     stacked = query_width // HEAD * fresh
-    span = ctx_count * capacity
     vm = pl.BlockSpec(memory_space=pltpu.VMEM)
-    sm = pl.BlockSpec(memory_space=pltpu.SMEM)
     hbm = pl.BlockSpec(memory_space=pl.ANY)
     dma = pltpu.SemaphoreType.DMA
     V = pltpu.VMEM
     lanes = exp_count * capacity
     pieces = 4
-    chunks = next(n for n in (3, 2, 1) if page_size % (16 * n) == 0 or n == 1)
+    halves = 2 if slab % 32 == 0 else 1
     context, layer_out = pl.pallas_call(
         functools.partial(fused_kernel, ctx_count, exp_count, capacity),
-        out_shape=(
-            jax.ShapeDtypeStruct((fresh, query_width), BF),
-            jax.ShapeDtypeStruct((rows, width), BF),
-        ),
-        in_specs=[sm, vm, hbm, vm, vm, vm, vm, hbm, hbm, hbm],
+        out_shape=(V((fresh, query_width), BF), V((rows, width), BF)),
+        in_specs=[hbm] * 10,
         out_specs=(vm, vm),
         scratch_shapes=[
-            V((ctx_count, chunks, page_size // chunks, 2 * HEAD), BF),
-            V((chunks, page_size // chunks) + pages.shape[2:], BF),
+            V((1, ctx_count), jnp.int32),
+            V((fresh, query_width), BF),
+            V((rows, width), BF),
+            V((1, width), F32),
+            V((top, rows), jnp.int32),
+            V((top, rows), F32),
+            V((ctx_count, halves, slab // halves) + pages.shape[2:], BF),
+            V((ctx_count, fresh) + pages.shape[2:], BF),
+            V((ctx_count, slab, 3 * HEAD), BF),
+            V((ctx_count * fresh, 3 * HEAD), BF),
             V((stacked, HEAD), BF),
-            V((fresh, page_size // chunks), F32),
             V((stacked, HEAD), F32),
-            V((stacked, HEAD), F32),
-            V((stacked, HEAD), F32),
+            V((stacked, 2 * HEAD), F32),
             V(out_weight.shape, BF),
             V(expert_input.shape[1:], BF),
             V((width, hidden_width), BF),
@@ -583,12 +655,12 @@
             V((ctx_count, rows, width), BF),
             V((exp_count, ctx_count, capacity, width), BF),
             V((exp_count, ctx_count, capacity, width), BF),
-            V((exp_count * span, width), F32),
             V((exp_count, ctx_count, capacity, width), BF),
             V((exp_count, ctx_count, capacity, width), BF),
             V((ctx_count, rows, width), BF),
             V((ctx_count, rows, width), BF),
-            dma((ctx_count, chunks)), dma((ctx_count, chunks)), dma((ctx_count, chunks)), dma((3,)),
+            dma((halves + 1,)), dma((6,)),
+            dma((ctx_count, halves + 1)), dma((ctx_count, halves + 1)), dma((ctx_count, halves + 1)), dma((3,)),
             dma((ctx_count,)), dma((ctx_count,)), dma((ctx_count,)), dma((ctx_count,)),
             dma((exp_count, pieces)), dma((exp_count, pieces)),
             dma((ctx_count,)), dma((ctx_count,)),
@@ -600,18 +672,9 @@
             collective_id=0, has_side_effects=True, vmem_limit_bytes=VMEM_LIMIT
         ),
     )(
-        cached_lengths[0], queries[0], pages[0], residual_in[0], norm_gain.reshape(1, width),
+        cached_lengths, queries[0], pages[0], residual_in[0], norm_gain.reshape(1, width),
         expert_ids[0].T, route_scores[0].T, out_weight, expert_input[0], expert_output[0],
     )
-    context, layer_out = pl.pallas_call(
-        settle,
-        out_shape=(
-            jax.ShapeDtypeStruct(context.shape, BF),
-            jax.ShapeDtypeStruct(layer_out.shape, BF),
-        ),
-        in_specs=[vm, vm],
-        out_specs=(vm, vm),
-    )(context, layer_out)
     return context[None], layer_out[None]
 
 

time: 67.5 us -> 54.9 us (0.81)
  Pallas kernels: 66.7 us -> 52.8 us
  local copies, waits for them, and re-layouts: 0 us -> 1.29 us
    pallas_call x1, Pallas kernels: 65.1 us -> 52.8 us  [fused_device(): pl.pallas_call(functools.partial(fused_kernel, ctx_count, exp_count, capa...]
    pallas_call x1 -> x0, Pallas kernels: 1.59 us -> none  [fused_device(): pl.pallas_call(settle, out_shape=(jax.ShapeDtypeStruct(context.shape, BF)...]
    unnamed x0 -> x2, local copies, waits for them, and re-layouts: none -> 1.29 us
where the time goes in v1:
time: 54.9 us; the launch traced here: 54.7 us
  Pallas kernels  52.8 us (96%)
  local copies, waits for them, and re-layouts  1.29 us (2%)
  between operations  0.64 us (1%)
    pallas_call x1, Pallas kernels, fused_device(): pl.pallas_call(functools.partial(fused_kernel, ctx_count, exp_count, capa...  52.8 us
    unnamed x2, local copies, waits for them, and re-layouts  1.29 us

profile of v1, /device:TPU:0, one launch (start us, length us, event | category | flops | bytes accessed | tf_op | source)
XLA Modules:
  0.0 54.7 jit_solution(8874899999144210227)
XLA Ops:
  0.6 52.8 %shard_map.113 = (bf16[64,1024]{1,0:T(8,128)(2,1)S(1)}, bf16[16,2048]{1,0:T(8,128)(2,1)S(1)}) custom-call(s32[1,4]{1,0:T(1,128)} %lengths.1, bf16[64,1024]{1,0:T(8,128)(2,1)} %bitcast.19, bf16[576,2,128]{2,1,0:T(2,128)(2,1)} %bitcast.18, bf16[16,2048]{1,0:T(8,128)(2,1)} %bitcast.20, f32[1,2048]{1,0:T(1,128)} %bitcast.21, s32[8,16]{1,0:T(8,128)} %bitcast.22, ...), custom_call_target="tpu_custom_call" | custom-call | tf_op jit(solution)/shard_map/pallas_call | solution.py:622
  53.5 0.7 %copy.14 = bf16[1,64,1024]{2,1,0:T(8,128)(2,1)} copy(bf16[1,64,1024]{2,1,0:T(8,128)(2,1)S(1)} %bitcast.14) | data formatting | bytes 262144
  54.1 0.6 %copy.15 = bf16[1,16,2048]{2,1,0:T(8,128)(2,1)} copy(bf16[1,16,2048]{2,1,0:T(8,128)(2,1)S(1)} %bitcast.15) | data formatting | bytes 131072

commit v2 on v1

--- a/solution.py
+++ b/solution.py
@@ -190,23 +190,33 @@
     lengths, query, page, residual_in, gain_in, ids_in, scores_in, w_out, w_in, w_down,
     context_out, layer_out,
     lens, q_in, residual, gain, ids, scores,
-    raw, raw_fresh, kv, kv_fresh, q_rows, peak, accum, wo, wi, wg, wu, wd,
+    raw, kv, kv_fresh, q_rows, peak, accum, part_send, part_recv, level_send, level_recv,
+    wo, wi, wg, wu, wd,
     ids_all, scores_all, combine_all, place, gather,
     rs_full, rs_send, rs_recv, hidden, nz, x_send, x_recv, y_send, y_recv, mix_send, mix_recv,
-    own_sem, in_sem, kv_left, kv_right, kv_recv, w_sem,
+    own_sem, in_sem, kv_send, kv_recv, w_sem, q_sem, part_sem,
     ids_s, ids_r, sc_s, sc_r, rs_s, rs_r, nz_s, nz_r, dx_s, dx_r, ret_s, ret_r, mix_s, mix_r,
 ):
     ci = lax.axis_index("ctx")
     ei = lax.axis_index("exp")
-    fresh = q_in.shape[0]
-    heads = q_in.shape[1] // HEAD
-    halves = raw.shape[1]
-    half_rows = raw.shape[2]
-    slab = halves * half_rows
+    fresh = q_in.shape[1]
+    heads = q_in.shape[2] // HEAD
+    slab = kv.shape[1]
+    halves = 2 if slab % 32 == 0 else 1
+    half_rows = slab // halves
     rows = residual.shape[0]
     width = residual.shape[1]
     top = ids.shape[0]
+    stacked = q_rows.shape[1]
     scaling = HEAD ** (-0.5) * 1.4426950408889634
+
+    last = ctx_count - 1
+    edge = (ci == 0) | (ci == last)
+    inner = (ci > 0) & (ci < last)
+    near_edge = jnp.where(ci < 2, 0, last)
+    across = last - ci
+    far_edge = last - near_edge
+    beside_edge = jnp.where(ci == 0, 1, last - 1)
 
     def ctx_peer(k):
         return {"ctx": lax.rem(ci + k, ctx_count)}
@@ -225,20 +235,12 @@
     for k in range(1, exp_count):
         pl.semaphore_signal(barrier, inc=1, device_id=exp_peer(k), device_id_type=MESH)
 
-    def page_piece(c):
-        return page.at[pl.ds(c * half_rows, half_rows)] if c < halves else page.at[pl.ds(slab, fresh)]
-
-    def raw_piece(p, c):
-        return raw.at[p, c] if c < halves else raw_fresh.at[p]
-
-    pieces_in_order = [halves] + list(range(halves))
-    own_page = [pltpu.make_async_copy(page_piece(c), raw_piece(ci, c), own_sem.at[c]) for c in range(halves + 1)]
-    for c in pieces_in_order:
-        own_page[c].start()
+    own_page = pltpu.make_async_copy(page, raw.at[ci], own_sem.at[0])
+    own_page.start()
     inputs = [
         pltpu.make_async_copy(src, dst, in_sem.at[n])
         for n, (src, dst) in enumerate(
-            [(lengths, lens), (query, q_in), (residual_in, residual), (gain_in, gain), (ids_in, ids), (scores_in, scores)]
+            [(lengths, lens), (query, q_in.at[0]), (residual_in, residual), (gain_in, gain), (ids_in, ids), (scores_in, scores)]
         )
     ]
     for c in inputs:
@@ -258,206 +260,264 @@
     peak[...] = jnp.full_like(peak, floor_value)
     pl.semaphore_wait(barrier, ctx_count + exp_count - 2)
 
-    def send_right(p, c, src):
-        dst = raw_piece(p, c) if isinstance(c, int) else raw.at[p, c]
-        return remote(src, dst, kv_right.at[p, c], kv_recv.at[p, c], {"ctx": ci + 1})
-
-    def send_left(p, c, src):
-        dst = raw_piece(p, c) if isinstance(c, int) else raw.at[p, c]
-        return remote(src, dst, kv_left.at[p, c], kv_recv.at[p, c], {"ctx": ci - 1})
-
     small = []
     for k in range(1, ctx_count):
-        small.append(remote(ids_in, ids_all.at[ci], ids_s.at[k], ids_r.at[ci], ctx_peer(k)))
-        small.append(remote(scores_in, scores_all.at[ci], sc_s.at[k], sc_r.at[ci], ctx_peer(k)))
+        small.append(remote(ids_in, ids_all.at[ci], ids_s.at[0], ids_r.at[0], ctx_peer(k)))
+        small.append(remote(scores_in, scores_all.at[ci], sc_s.at[0], sc_r.at[0], ctx_peer(k)))
     for c in small:
         c.start()
 
-    for c in pieces_in_order:
-        @pl.when(ci < ctx_count - 1)
-        def _():
-            send_right(ci, c, page_piece(c)).start()
-
-        if c < halves:
-            @pl.when(ci > 0)
-            def _():
-                send_left(ci, c, page_piece(c)).start()
+    def rows_of(c):
+        return pl.ds(c * half_rows, half_rows) if c < halves else pl.ds(slab, fresh)
+
+    def piece(p, c, src, sem, step):
+        return remote(src.at[rows_of(c)], raw.at[p, rows_of(c)], kv_send.at[sem], kv_recv.at[p, c], {"ctx": ci + step})
+
+    order_right = [halves] + list(range(halves))
+    order_left = list(range(halves))
+
+    @pl.when(ci < last)
+    def _():
+        for c in order_right:
+            piece(ci, c, page, 0, 1).start()
+
+    @pl.when(ci > 0)
+    def _():
+        for c in order_left:
+            piece(ci, c, page, 1, -1).start()
+
+    def query_copy(where):
+        return remote(query, q_in.at[1], q_sem.at[0], q_sem.at[1], {"ctx": where})
+
+    @pl.when(edge)
+    def _():
+        query_copy(beside_edge).start()
+
+    def stage_queries(n):
+        for h in range(heads):
+            q_rows[n, h * fresh:(h + 1) * fresh, :] = q_in[n, :, h * HEAD:(h + 1) * HEAD]
 
     inputs[0].wait()
     inputs[1].wait()
-    for h in range(heads):
-        q_rows[h * fresh:(h + 1) * fresh, :] = q_in[:, h * HEAD:(h + 1) * HEAD]
+    stage_queries(0)
 
     step = next(n for n in (4, 2, 1) if heads % n == 0)
     page_number = lax.broadcasted_iota(jnp.int32, (1, ctx_count), 1)
     slab_row = lax.broadcasted_iota(jnp.int32, (1, slab), 1).astype(F32)
 
     def split(p, c):
-        both = pltpu.einshape("sgh->gsh", raw[p, c])
-        at = pl.ds(pl.multiple_of(c * half_rows, half_rows), half_rows)
-        kv[p, at, :HEAD] = both[0]
-        kv[p, at, HEAD:2 * HEAD] = both[1]
-
-    def split_fresh(p):
-        both = pltpu.einshape("sgh->gsh", raw_fresh[p])
-        at = pl.ds(pl.multiple_of(p * fresh, fresh), fresh)
-        kv_fresh[at, :HEAD] = both[0]
-        kv_fresh[at, HEAD:2 * HEAD] = both[1]
-
-    def attend(source, bias):
+        both = pltpu.einshape("sgh->gsh", raw[p, rows_of(c)])
+        if c < halves:
+            kv[p, rows_of(c), :HEAD] = both[0]
+            kv[p, rows_of(c), HEAD:2 * HEAD] = both[1]
+        else:
+            at = pl.ds(pl.multiple_of(p * fresh, fresh), fresh)
+            kv_fresh[at, :HEAD] = both[0]
+            kv_fresh[at, HEAD:2 * HEAD] = both[1]
+
+    def attend(n, source, bias):
         keys = source[:, :HEAD]
         values = source[:, HEAD:]
         count = keys.shape[0]
         for h in range(0, heads, step):
             sl = slice(h * fresh, (h + step) * fresh)
             s = lax.dot_general(
-                q_rows[sl, :], keys, (((1,), (1,)), ((), ())), preferred_element_type=F32
+                q_rows[n, sl, :], keys, (((1,), (1,)), ((), ())), preferred_element_type=F32
             )
             s = (s.reshape(step, fresh, count) + bias[None]).reshape(step * fresh, count)
-            old = peak[sl, :]
+            old = peak[n, sl, :]
             now = jnp.maximum(old, jnp.max(s, axis=1, keepdims=True))
             w = jnp.exp2((s - now[:, :1]) * scaling)
             fade = jnp.exp2((old - now) * scaling)
-            accum[sl, :] = accum[sl, :] * jnp.concatenate([fade, fade], 1) + jnp.dot(
+            accum[n, sl, :] = accum[n, sl, :] * jnp.concatenate([fade, fade], 1) + jnp.dot(
                 w.astype(BF), values, preferred_element_type=F32
             )
-            peak[sl, :] = now
-
-    def attend_page(p):
+            peak[n, sl, :] = now
+
+    def attend_page(n, p):
         live = jnp.sum(jnp.where(page_number == p, lens[...], 0).astype(F32), axis=1, keepdims=True)
-        attend(kv.at[p], jnp.where(slab_row < live, 0.0, floor_value))
-
-    def attend_fresh():
-        count = kv_fresh.shape[0]
-        position = lax.broadcasted_iota(jnp.int32, (fresh, count), 0) + ci * fresh
-        attend(kv_fresh, jnp.where(lax.broadcasted_iota(jnp.int32, (fresh, count), 1) <= position, 0.0, floor_value))
-
-    own_page[halves].wait()
-    split_fresh(ci)
-    for c in range(halves):
-        own_page[c].wait()
+        attend(n, kv.at[p], jnp.where(slab_row < live, 0.0, floor_value))
+
+    def attend_fresh(n, home, first, count):
+        count *= fresh
+        at = pl.ds(pl.multiple_of(first * fresh, fresh), count)
+        row = lax.broadcasted_iota(jnp.int32, (fresh, count), 1) + first * fresh
+        position = lax.broadcasted_iota(jnp.int32, (fresh, count), 0) + home * fresh
+        attend(n, kv_fresh.at[at], jnp.where(row <= position, 0.0, floor_value))
+
+    own_page.wait()
+    for c in order_right:
         split(ci, c)
-    attend_page(ci)
-
-    steps = 2 * halves * (ctx_count - 1)
-    depth = next(n for n in range(-(-width // (steps + 4)), width + 1) if width % n == 0 and n % 16 == 0)
-    blocks = width // depth
+    attend_page(0, ci)
+
+    depth = next(n for n in (256, 128, 64, 32, 16) if width % n == 0)
     copies_w[1].wait()
 
-    def unpack(i):
+    def unpack(i, carry):
         at = pl.ds(pl.multiple_of(i * depth, depth), depth)
         block = pltpu.einshape("dgh->gdh", wi[at])
         wg[at, :] = block[0]
         wu[at, :] = block[1]
-
-    ahead = max(0, blocks - steps)
-    for i in range(ahead):
-        unpack(i)
+        return carry
+
+    lax.fori_loop(0, width // depth, unpack, 0)
 
     for c in inputs[2:]:
         c.wait()
     ids_all[ci] = ids[...]
     scores_all[ci] = scores[...]
-    for k in range(1, ctx_count):
-        source = lax.rem(ci + k, ctx_count)
-        remote(ids_in, ids_all.at[source], ids_s.at[k], ids_r.at[source], ctx_peer(k)).wait_recv()
-        remote(scores_in, scores_all.at[source], sc_s.at[k], sc_r.at[source], ctx_peer(k)).wait_recv()
-    for k in range(ctx_count):
-        given = scores_all[k]
-        combine_all[k] = (given / jnp.sum(given, axis=0, keepdims=True)).astype(BF).astype(F32)
-
-    lanes = exp_count * capacity
-    lane = lax.broadcasted_iota(jnp.int32, (lanes, rows), 0)
-    wanted = ci * exp_count + lax.rem(ei + lane // capacity, exp_count)
-    seat = (lane - lane // capacity * capacity).astype(F32)
-    earlier = (
-        lax.broadcasted_iota(jnp.int32, (rows, rows), 0)
-        < lax.broadcasted_iota(jnp.int32, (rows, rows), 1)
-    ).astype(F32)
-    for k in range(ctx_count):
-        chosen = jnp.zeros((lanes, rows), F32)
-        portion = jnp.zeros((lanes, rows), F32)
-        for j in range(top):
-            hit = ids_all[k, j:j + 1, :] == wanted
-            chosen = jnp.where(hit, 1.0, chosen)
-            portion = jnp.where(hit, combine_all[k, j:j + 1, :], portion)
-        rank = jnp.dot(chosen.astype(BF), earlier.astype(BF), preferred_element_type=F32)
-        seated = (chosen > 0.5) & (rank == seat)
-        place[k] = jnp.where(seated, 1.0, 0.0)
-        gather[k] = jnp.where(seated, portion, 0.0)
-
-    def pass_on(p, c):
-        src = raw_piece(p, c) if isinstance(c, int) else raw.at[p, c]
-
-        @pl.when((p < ci) & (ci < ctx_count - 1))
+
+    def route():
+        others = pl.ds(0, last)
+        remote(ids_all.at[others], ids_all.at[others], ids_s.at[0], ids_r.at[0], ctx_peer(1)).wait_recv()
+        remote(scores_all.at[others], scores_all.at[others], sc_s.at[0], sc_r.at[0], ctx_peer(1)).wait_recv()
+        lanes = exp_count * capacity
+        lane = lax.broadcasted_iota(jnp.int32, (lanes, rows), 0)
+        wanted = ci * exp_count + lax.rem(ei + lane // capacity, exp_count)
+        seat = (lane - lane // capacity * capacity).astype(F32)
+        earlier = (
+            lax.broadcasted_iota(jnp.int32, (rows, rows), 0)
+            < lax.broadcasted_iota(jnp.int32, (rows, rows), 1)
+        ).astype(F32)
+        for k in range(ctx_count):
+            given = scores_all[k]
+            combine_all[k] = (given / jnp.sum(given, axis=0, keepdims=True)).astype(BF).astype(F32)
+        for k in range(ctx_count):
+            chosen = jnp.zeros((lanes, rows), F32)
+            portion = jnp.zeros((lanes, rows), F32)
+            for j in range(top):
+                hit = ids_all[k, j:j + 1, :] == wanted
+                chosen = jnp.where(hit, 1.0, chosen)
+                portion = jnp.where(hit, combine_all[k, j:j + 1, :], portion)
+            rank = jnp.dot(chosen.astype(BF), earlier.astype(BF), preferred_element_type=F32)
+            seated = (chosen > 0.5) & (rank == seat)
+            place[k] = jnp.where(seated, 1.0, 0.0)
+            gather[k] = jnp.where(seated, portion, 0.0)
+
+    def arrive(p, c):
+        piece(p, c, raw.at[p], 0, 1).wait_recv()
+
+    def pass_on(c):
+        @pl.when(ci < across)
         def _():
-            send_right(p, c, src).start()
-
-        if not (isinstance(c, int) and c == halves):
-            @pl.when((p > ci) & (ci > 0))
+            piece(near_edge, c, raw.at[near_edge], 2, 1).start()
+
+        if c < halves:
+            @pl.when(ci > across)
             def _():
-                send_left(p, c, src).start()
-
-    def arrival(i, carry):
-        d = i // (2 * halves) + 1
-        c = lax.rem(i // 2, halves)
-        p = jnp.where(lax.rem(i, 2) == 0, ci - d, ci + d)
-
-        @pl.when((p >= 0) & (p < ctx_count))
+                piece(near_edge, c, raw.at[near_edge], 2, -1).start()
+
+    def arrive_fresh(p):
+        arrive(p, halves)
+        split(p, halves)
+
+    block_rows = stacked // level_send.shape[0]
+
+    def part_copies(where):
+        return (
+            remote(part_send, part_recv, part_sem.at[0], part_sem.at[1], {"ctx": where}),
+            remote(level_send, level_recv, part_sem.at[2], part_sem.at[3], {"ctx": where}),
+        )
+
+    @pl.when(inner)
+    def _():
+        @pl.when(ci < across)
         def _():
-            @pl.when((c == 0) & (p < ci))
-            def _():
-                send_right(p, halves, raw_fresh.at[p]).wait_recv()
-                pass_on(p, halves)
-                split_fresh(p)
-
-            send_right(p, c, raw.at[p, c]).wait_recv()
-            pass_on(p, c)
-            split(p, c)
-
-            @pl.when(c == halves - 1)
-            def _():
-                attend_page(p)
-
-        @pl.when(i == jnp.maximum(ci - 1, 0) * 2 * halves)
+            arrive(near_edge, halves)
+            pass_on(halves)
+            split(near_edge, halves)
+
+        @pl.when(ci > across)
         def _():
-            attend_fresh()
-
-        @pl.when(i + ahead < blocks)
+            arrive_fresh(across)
+
+        for c in range(halves):
+            arrive(near_edge, c)
+            pass_on(c)
+            split(near_edge, c)
+            if c == 0:
+                route()
+            arrive(across, c)
+            split(across, c)
+        attend_page(0, near_edge)
+        attend_page(0, across)
+        query_copy(ci).wait_recv()
+        stage_queries(1)
+        attend_page(1, across)
+
+        @pl.when(ci > across)
         def _():
-            unpack(i + ahead)
-
-        return carry
-
-    lax.fori_loop(0, steps, arrival, 0)
-
-    for h in range(heads):
-        sl = slice(h * fresh, (h + 1) * fresh)
-        context_out[:, h * HEAD:(h + 1) * HEAD] = (accum[sl, :HEAD] / accum[sl, HEAD:]).astype(BF)
+            arrive_fresh(far_edge)
+            attend_fresh(1, near_edge, 0, ctx_count // 2)
+
+        attend_fresh(0, ci, 0, ctx_count)
+        for c in range(halves):
+            arrive(far_edge, c)
+            split(far_edge, c)
+        attend_page(1, far_edge)
+        for b in range(stacked // block_rows):
+            sl = slice(b * block_rows, (b + 1) * block_rows)
+            whole = accum[1, sl, HEAD:]
+            part_send[sl, :] = (accum[1, sl, :HEAD] / whole).astype(BF)
+            level = peak[1, sl, :] * scaling + jnp.log(whole) * 1.4426950408889634
+            level_send[b:b + 1, :] = jnp.transpose(level)[:1, :]
+        for c in part_copies(near_edge):
+            c.start()
+        attend_page(0, far_edge)
+        for h in range(heads):
+            sl = slice(h * fresh, (h + 1) * fresh)
+            context_out[:, h * HEAD:(h + 1) * HEAD] = (accum[0, sl, :HEAD] / accum[0, sl, HEAD:]).astype(BF)
+
+    @pl.when(edge)
+    def _():
+        route()
+
+        @pl.when(ci > 0)
+        def _():
+            arrive_fresh(beside_edge)
+
+        attend_fresh(0, ci, jnp.where(ci == 0, 0, ctx_count // 2), ctx_count // 2)
+        for c in range(halves):
+            arrive(beside_edge, c)
+            split(beside_edge, c)
+        attend_page(0, beside_edge)
+        for c in part_copies(ci):
+            c.wait_recv()
+        per = block_rows // fresh
+        for b in range(stacked // block_rows):
+            sl = slice(b * block_rows, (b + 1) * block_rows)
+            theirs = jnp.transpose(jnp.broadcast_to(level_recv[b:b + 1, :], (HEAD, block_rows)))
+            ours = peak[0, sl, :] * scaling
+            level = jnp.maximum(ours, theirs)
+            fade = jnp.exp2(ours - level)
+            share = jnp.exp2(theirs - level)
+            merged = (accum[0, sl, :HEAD] * fade + part_recv[sl, :].astype(F32) * share) / (
+                accum[0, sl, HEAD:] * fade + share
+            )
+            for h in range(per):
+                at = b * per + h
+                context_out[:, at * HEAD:(at + 1) * HEAD] = merged[h * fresh:(h + 1) * fresh, :].astype(BF)
 
     copies_w[0].wait()
 
     pieces = 4
-    piece = width // pieces
-    own_share = []
-    rs_copies = []
+    piece_width = width // pieces
+    senders = pl.ds(1, exp_count - 1)
     for n in range(pieces):
-        cols = slice(n * piece, (n + 1) * piece)
+        cols = slice(n * piece_width, (n + 1) * piece_width)
         part = jnp.dot(context_out[...], wo[:, cols], preferred_element_type=F32)
         rs_full[n] = part
         for k in range(1, exp_count):
             at = pl.ds(pl.multiple_of(lax.rem(ei + k, exp_count) * rows, rows), rows)
             rs_send[k, n] = rs_full[n, at, :].astype(BF)
-            c = remote(rs_send.at[k, n], rs_recv.at[k, n], rs_s.at[k, n], rs_r.at[k, n], exp_peer(k))
-            c.start()
-            rs_copies.append(c)
+            remote(rs_send.at[k, n], rs_recv.at[k, n], rs_s.at[0], rs_r.at[n], exp_peer(k)).start()
     mine = pl.ds(pl.multiple_of(ei * rows, rows), rows)
     square = jnp.zeros((rows, 1), F32)
     for n in range(pieces):
-        cols = slice(n * piece, (n + 1) * piece)
+        cols = slice(n * piece_width, (n + 1) * piece_width)
         share = rs_full[n, mine, :]
+        remote(rs_send.at[senders, n], rs_recv.at[senders, n], rs_s.at[0], rs_r.at[n], exp_peer(1)).wait_recv()
         for k in range(1, exp_count):
-            rs_copies[n * (exp_count - 1) + k - 1].wait_recv()
             share = share + rs_recv[k, n].astype(F32)
         h = (residual[:, cols].astype(F32) + share).astype(BF)
         hidden[:, cols] = h
@@ -466,7 +526,6 @@
     inverse = lax.rsqrt(square / width + norm_epsilon)
     nz[ci] = (hidden[...].astype(F32) * inverse * gain[...]).astype(BF)
 
-    last = ctx_count - 1
     middle = last / 2
     send_table, work_table = [], []
     for c in range(ctx_count):
@@ -480,33 +539,30 @@
             value = jnp.where(ci == c, table[c][n], value)
         return value
 
-    def nz_copy(p, n, where):
-        return remote(nz.at[p], nz.at[p], nz_s.at[n], nz_r.at[p], {"ctx": where})
-
-    nz_copies = []
+    def nz_copy(p, where):
+        return remote(nz.at[p], nz.at[p], nz_s.at[0], nz_r.at[p], {"ctx": where})
+
     for n in range(last):
-        c = nz_copy(ci, n, lookup(send_table, n))
-        c.start()
-        nz_copies.append(c)
+        nz_copy(ci, lookup(send_table, n)).start()
 
     places = [lookup(work_table, n) for n in range(ctx_count)]
 
     def dx_copy(j, n):
         p = places[n]
-        return remote(x_send.at[j, p], x_recv.at[j, p], dx_s.at[j, p], dx_r.at[j, p], exp_peer(j))
+        return remote(x_send.at[j, p], x_recv.at[j, p], dx_s.at[0], dx_r.at[p], exp_peer(1 if j is senders else j))
 
     def ret_copy(j, n):
         p = places[n]
-        return remote(y_send.at[j, p], y_recv.at[j, p], ret_s.at[j, p], ret_r.at[j, p], exp_peer(exp_count - j))
+        return remote(y_send.at[j, p], y_recv.at[j, p], ret_s.at[0], ret_r.at[p], exp_peer(1 if j is senders else exp_count - j))
 
     def mix_copy(n):
         p = places[n]
-        return remote(mix_send.at[p], mix_recv.at[ci], mix_s.at[p], mix_r.at[ci], {"ctx": p})
+        return remote(mix_send.at[p], mix_recv.at[ci], mix_s.at[0], mix_r.at[ci], {"ctx": p})
 
     def dispatch(n):
         p = places[n]
         if n:
-            nz_copy(p, 0, p).wait_recv()
+            nz_copy(p, p).wait_recv()
         routed = jnp.dot(place[p].astype(BF), nz[p], preferred_element_type=F32)
         for j in list(range(1, exp_count)) + [0]:
             block = routed[j * capacity:(j + 1) * capacity].astype(BF)
@@ -518,8 +574,7 @@
 
     def experts(n):
         p = places[n]
-        for j in range(1, exp_count):
-            dx_copy(j, n).wait_recv()
+        dx_copy(senders, n).wait_recv()
         x = jnp.concatenate([x_recv[j, p].astype(F32) for j in range(exp_count)], 0).astype(BF)
         gate = jnp.dot(x, wg[...], preferred_element_type=F32)
         up = jnp.dot(x, wu[...], preferred_element_type=F32)
@@ -535,8 +590,7 @@
 
     def mixing(n):
         p = places[n]
-        for j in range(1, exp_count):
-            ret_copy(j, n).wait_recv()
+        ret_copy(senders, n).wait_recv()
         rows_p = jnp.concatenate([y_recv[j, p].astype(F32) for j in range(exp_count)], 0).astype(BF)
         mixed = lax.dot_general(
             gather[p].astype(BF), rows_p, (((0,), (0,)), ((), ())), preferred_element_type=F32
@@ -560,43 +614,52 @@
     out = hidden[...].astype(F32) + mixing(0)
     for n in range(1, ctx_count):
         p = places[n]
-        remote(mix_send.at[p], mix_recv.at[p], mix_s.at[p], mix_r.at[p], {"ctx": p}).wait_recv()
+        remote(mix_send.at[p], mix_recv.at[p], mix_s.at[0], mix_r.at[p], {"ctx": p}).wait_recv()
         out = out + mix_recv[p].astype(F32)
     layer_out[...] = out.astype(BF)
 
-    for c in rs_copies + nz_copies + small:
-        c.wait_send()
-    for n in range(ctx_count):
-        for j in range(1, exp_count):
-            dx_copy(j, n).wait_send()
-            ret_copy(j, n).wait_send()
-        if n:
-            mix_copy(n).wait_send()
-
-    for c in pieces_in_order:
-        @pl.when(ci < ctx_count - 1)
+    others = pl.ds(0, last)
+    for src, dst, sem in [
+        (ids_all.at[others], ids_all.at[others], ids_s), (scores_all.at[others], scores_all.at[others], sc_s),
+        (nz.at[others], nz.at[others], nz_s), (mix_send.at[others], mix_recv.at[others], mix_s),
+    ]:
+        remote(src, dst, sem.at[0], mix_r.at[0], ctx_peer(1)).wait_send()
+    for src, dst, sem in [
+        (rs_send.at[senders], rs_recv.at[senders], rs_s), (x_send.at[senders], x_recv.at[senders], dx_s),
+        (y_send.at[senders], y_recv.at[senders], ret_s),
+    ]:
+        remote(src, dst, sem.at[0], mix_r.at[0], exp_peer(1)).wait_send()
+
+    everything = pl.ds(0, slab + fresh)
+    cached = pl.ds(0, slab)
+
+    def sent(at, sem):
+        remote(raw.at[0, at], raw.at[0, at], kv_send.at[sem], kv_recv.at[0, 0], ctx_peer(1)).wait_send()
+
+    @pl.when(ci < last)
+    def _():
+        sent(everything, 0)
+
+    @pl.when(ci > 0)
+    def _():
+        sent(cached, 1)
+
+    @pl.when(edge)
+    def _():
+        query_copy(beside_edge).wait_send()
+
+    @pl.when(inner)
+    def _():
+        @pl.when(ci < across)
         def _():
-            send_right(ci, c, page_piece(c)).wait_send()
-
-        if c < halves:
-            @pl.when(ci > 0)
-            def _():
-                send_left(ci, c, page_piece(c)).wait_send()
-
-    def drain(p, carry):
-        for c in pieces_in_order:
-            @pl.when((p < ci) & (ci < ctx_count - 1))
-            def _():
-                send_right(p, c, raw_piece(p, c)).wait_send()
-
-            if c < halves:
-                @pl.when((p > ci) & (ci > 0))
-                def _():
-                    send_left(p, c, raw_piece(p, c)).wait_send()
-
-        return carry
-
-    lax.fori_loop(0, ctx_count, drain, 0)
+            sent(everything, 2)
+
+        @pl.when(ci > across)
+        def _():
+            sent(cached, 2)
+
+        for c in part_copies(near_edge):
+            c.wait_send()
 
 
 def fused_device(
@@ -619,6 +682,7 @@
     lanes = exp_count * capacity
     pieces = 4
     halves = 2 if slab % 32 == 0 else 1
+    blocks = stacked // HEAD
     context, layer_out = pl.pallas_call(
         functools.partial(fused_kernel, ctx_count, exp_count, capacity),
         out_shape=(V((fresh, query_width), BF), V((rows, width), BF)),
@@ -626,18 +690,21 @@
         out_specs=(vm, vm),
         scratch_shapes=[
             V((1, ctx_count), jnp.int32),
-            V((fresh, query_width), BF),
+            V((2, fresh, query_width), BF),
             V((rows, width), BF),
             V((1, width), F32),
             V((top, rows), jnp.int32),
             V((top, rows), F32),
-            V((ctx_count, halves, slab // halves) + pages.shape[2:], BF),
-            V((ctx_count, fresh) + pages.shape[2:], BF),
+            V((ctx_count,) + pages.shape[1:], BF),
             V((ctx_count, slab, 3 * HEAD), BF),
             V((ctx_count * fresh, 3 * HEAD), BF),
+            V((2, stacked, HEAD), BF),
+            V((2, stacked, HEAD), F32),
+            V((2, stacked, 2 * HEAD), F32),
             V((stacked, HEAD), BF),
-            V((stacked, HEAD), F32),
-            V((stacked, 2 * HEAD), F32),
+            V((stacked, HEAD), BF),
+            V((blocks, HEAD), F32),
+            V((blocks, HEAD), F32),
             V(out_weight.shape, BF),
             V(expert_input.shape[1:], BF),
             V((width, hidden_width), BF),
@@ -659,14 +726,9 @@
             V((exp_count, ctx_count, capacity, width), BF),
             V((ctx_count, rows, width), BF),
             V((ctx_count, rows, width), BF),
-            dma((halves + 1,)), dma((6,)),
-            dma((ctx_count, halves + 1)), dma((ctx_count, halves + 1)), dma((ctx_count, halves + 1)), dma((3,)),
-            dma((ctx_count,)), dma((ctx_count,)), dma((ctx_count,)), dma((ctx_count,)),
-            dma((exp_count, pieces)), dma((exp_count, pieces)),
-            dma((ctx_count,)), dma((ctx_count,)),
-            dma((exp_count, ctx_count)), dma((exp_count, ctx_count)),
-            dma((exp_count, ctx_count)), dma((exp_count, ctx_count)),
-            dma((ctx_count,)), dma((ctx_count,)),
+            dma((1,)), dma((6,)), dma((3,)), dma((ctx_count, halves + 1)), dma((3,)), dma((2,)), dma((4,)),
+            dma((1,)), dma((1,)), dma((1,)), dma((1,)), dma((1,)), dma((pieces,)), dma((1,)), dma((ctx_count,)),
+            dma((1,)), dma((ctx_count,)), dma((1,)), dma((ctx_count,)), dma((1,)), dma((ctx_count,)),
         ],
         compiler_params=pltpu.CompilerParams(
             collective_id=0, has_side_effects=True, vmem_limit_bytes=VMEM_LIMIT
@@ -679,7 +741,7 @@
 
 
 def fused_fits(mesh):
-    return mesh.shape["rep"] == 1 and mesh.shape["ctx"] <= 8
+    return mesh.shape["rep"] == 1 and mesh.shape["ctx"] == 4
 
 
 def solution(mesh):

time: 54.9 us -> 53.1 us (0.967)
  Pallas kernels: 52.8 us -> 51 us
    pallas_call x1, Pallas kernels: 52.8 us -> 51 us  [fused_device(): pl.pallas_call(functools.partial(fused_kernel, ctx_count, exp_count, capa...]
where the time goes in v2:
time: 53.1 us; the launch traced here: 52.9 us
  Pallas kernels  51 us (96%)
  local copies, waits for them, and re-layouts  1.29 us (2%)
  between operations  0.64 us (1%)
    pallas_call x1, Pallas kernels, fused_device(): pl.pallas_call(functools.partial(fused_kernel, ctx_count, exp_count, capa...  51 us
    unnamed x2, local copies, waits for them, and re-layouts  1.29 us

profile of v2, /device:TPU:0, one launch (start us, length us, event | category | flops | bytes accessed | tf_op | source)
XLA Modules:
  0.0 52.9 jit_solution(2930216979175628350)
XLA Ops:
  0.6 51.0 %shard_map.113 = (bf16[64,1024]{1,0:T(8,128)(2,1)S(1)}, bf16[16,2048]{1,0:T(8,128)(2,1)S(1)}) custom-call(s32[1,4]{1,0:T(1,128)} %lengths.1, bf16[64,1024]{1,0:T(8,128)(2,1)} %bitcast.19, bf16[576,2,128]{2,1,0:T(2,128)(2,1)} %bitcast.18, bf16[16,2048]{1,0:T(8,128)(2,1)} %bitcast.20, f32[1,2048]{1,0:T(1,128)} %bitcast.21, s32[8,16]{1,0:T(8,128)} %bitcast.22, ...), custom_call_target="tpu_custom_call" | custom-call | tf_op jit(solution)/shard_map/pallas_call | solution.py:686
  51.6 0.7 %copy.14 = bf16[1,64,1024]{2,1,0:T(8,128)(2,1)} copy(bf16[1,64,1024]{2,1,0:T(8,128)(2,1)S(1)} %bitcast.14) | data formatting | bytes 262144
  52.3 0.6 %copy.15 = bf16[1,16,2048]{2,1,0:T(8,128)(2,1)} copy(bf16[1,16,2048]{2,1,0:T(8,128)(2,1)S(1)} %bitcast.15) | data formatting | bytes 131072

commit v3 on v2

--- a/solution.py
+++ b/solution.py
@@ -194,7 +194,7 @@
     wo, wi, wg, wu, wd,
     ids_all, scores_all, combine_all, place, gather,
     rs_full, rs_send, rs_recv, hidden, nz, x_send, x_recv, y_send, y_recv, mix_send, mix_recv,
-    own_sem, in_sem, kv_send, kv_recv, w_sem, q_sem, part_sem,
+    own_sem, in_sem, kv_send, kv_recv, w_sem, q_sem, part_sem, entered,
     ids_s, ids_r, sc_s, sc_r, rs_s, rs_r, nz_s, nz_r, dx_s, dx_r, ret_s, ret_r, mix_s, mix_r,
 ):
     ci = lax.axis_index("ctx")
@@ -230,10 +230,17 @@
         )
 
     barrier = pltpu.get_barrier_semaphore()
-    for k in range(1, ctx_count):
-        pl.semaphore_signal(barrier, inc=1, device_id=ctx_peer(k), device_id_type=MESH)
+
+    @pl.when(inner)
+    def _():
+        for where in (across, near_edge):
+            pl.semaphore_signal(barrier, inc=1, device_id={"ctx": where}, device_id_type=MESH)
+
     for k in range(1, exp_count):
         pl.semaphore_signal(barrier, inc=1, device_id=exp_peer(k), device_id_type=MESH)
+
+    def tell(n, where):
+        pl.semaphore_signal(entered.at[n], inc=1, device_id={"ctx": where}, device_id_type=MESH)
 
     own_page = pltpu.make_async_copy(page, raw.at[ci], own_sem.at[0])
     own_page.start()
@@ -258,14 +265,11 @@
     kv_fresh[:, 2 * HEAD:] = jnp.ones((kv_fresh.shape[0], HEAD), BF)
     accum[...] = jnp.zeros_like(accum)
     peak[...] = jnp.full_like(peak, floor_value)
-    pl.semaphore_wait(barrier, ctx_count + exp_count - 2)
-
-    small = []
-    for k in range(1, ctx_count):
-        small.append(remote(ids_in, ids_all.at[ci], ids_s.at[0], ids_r.at[0], ctx_peer(k)))
-        small.append(remote(scores_in, scores_all.at[ci], sc_s.at[0], sc_r.at[0], ctx_peer(k)))
-    for c in small:
-        c.start()
+    pl.semaphore_wait(barrier, exp_count)
+
+    def send_small(where):
+        remote(ids_in, ids_all.at[ci], ids_s.at[0], ids_r.at[0], {"ctx": where}).start()
+        remote(scores_in, scores_all.at[ci], sc_s.at[0], sc_r.at[0], {"ctx": where}).start()
 
     def rows_of(c):
         return pl.ds(c * half_rows, half_rows) if c < halves else pl.ds(slab, fresh)
@@ -276,13 +280,11 @@
     order_right = [halves] + list(range(halves))
     order_left = list(range(halves))
 
-    @pl.when(ci < last)
-    def _():
+    def send_right():
         for c in order_right:
             piece(ci, c, page, 0, 1).start()
 
-    @pl.when(ci > 0)
-    def _():
+    def send_left():
         for c in order_left:
             piece(ci, c, page, 1, -1).start()
 
@@ -291,7 +293,42 @@
 
     @pl.when(edge)
     def _():
+        tell(0, beside_edge)
+        send_small(beside_edge)
+
+        @pl.when(ci == 0)
+        def _():
+            send_right()
+
+        @pl.when(ci > 0)
+        def _():
+            send_left()
+
         query_copy(beside_edge).start()
+
+    @pl.when(inner)
+    def _():
+        send_small(across)
+
+        @pl.when(ci < across)
+        def _():
+            send_right()
+
+        @pl.when(ci > across)
+        def _():
+            send_left()
+
+        pl.semaphore_wait(entered.at[0], 1)
+        tell(1, across)
+        send_small(near_edge)
+
+        @pl.when(ci < across)
+        def _():
+            send_left()
+
+        @pl.when(ci > across)
+        def _():
+            send_right()
 
     def stage_queries(n):
         for h in range(heads):
@@ -315,7 +352,7 @@
             kv_fresh[at, :HEAD] = both[0]
             kv_fresh[at, HEAD:2 * HEAD] = both[1]
 
-    def attend(n, source, bias):
+    def attend(n, source, bias, after=None):
         keys = source[:, :HEAD]
         values = source[:, HEAD:]
         count = keys.shape[0]
@@ -333,10 +370,12 @@
                 w.astype(BF), values, preferred_element_type=F32
             )
             peak[n, sl, :] = now
-
-    def attend_page(n, p):
+            if after:
+                after(sl)
+
+    def attend_page(n, p, after=None):
         live = jnp.sum(jnp.where(page_number == p, lens[...], 0).astype(F32), axis=1, keepdims=True)
-        attend(n, kv.at[p], jnp.where(slab_row < live, 0.0, floor_value))
+        attend(n, kv.at[p], jnp.where(slab_row < live, 0.0, floor_value), after)
 
     def attend_fresh(n, home, first, count):
         count *= fresh
@@ -361,6 +400,18 @@
         return carry
 
     lax.fori_loop(0, width // depth, unpack, 0)
+
+    @pl.when(inner)
+    def _():
+        pl.semaphore_wait(entered.at[1], 1)
+        tell(2, near_edge)
+        send_small(far_edge)
+
+    @pl.when(edge)
+    def _():
+        pl.semaphore_wait(entered.at[2], 1)
+        send_small(last - beside_edge)
+        send_small(far_edge)
 
     for c in inputs[2:]:
         c.wait()
@@ -413,11 +464,11 @@
 
     block_rows = stacked // level_send.shape[0]
 
-    def part_copies(where):
-        return (
-            remote(part_send, part_recv, part_sem.at[0], part_sem.at[1], {"ctx": where}),
-            remote(level_send, level_recv, part_sem.at[2], part_sem.at[3], {"ctx": where}),
-        )
+    def part_copy(sl, where):
+        return remote(part_send.at[sl], part_recv.at[sl], part_sem.at[0], part_sem.at[1], {"ctx": where})
+
+    def level_copy(where):
+        return remote(level_send, level_recv, part_sem.at[2], part_sem.at[3], {"ctx": where})
 
     @pl.when(inner)
     def _():
@@ -435,8 +486,6 @@
             arrive(near_edge, c)
             pass_on(c)
             split(near_edge, c)
-            if c == 0:
-                route()
             arrive(across, c)
             split(across, c)
         attend_page(0, near_edge)
@@ -451,18 +500,22 @@
             attend_fresh(1, near_edge, 0, ctx_count // 2)
 
         attend_fresh(0, ci, 0, ctx_count)
+        route()
         for c in range(halves):
             arrive(far_edge, c)
             split(far_edge, c)
-        attend_page(1, far_edge)
-        for b in range(stacked // block_rows):
-            sl = slice(b * block_rows, (b + 1) * block_rows)
-            whole = accum[1, sl, HEAD:]
-            part_send[sl, :] = (accum[1, sl, :HEAD] / whole).astype(BF)
-            level = peak[1, sl, :] * scaling + jnp.log(whole) * 1.4426950408889634
-            level_send[b:b + 1, :] = jnp.transpose(level)[:1, :]
-        for c in part_copies(near_edge):
-            c.start()
+
+        def finish(sl):
+            for b in range(sl.start // block_rows, sl.stop // block_rows):
+                at = slice(b * block_rows, (b + 1) * block_rows)
+                whole = accum[1, at, HEAD:]
+                part_send[at, :] = (accum[1, at, :HEAD] / whole).astype(BF)
+                level = peak[1, at, :] * scaling + jnp.log(whole) * 1.4426950408889634
+                level_send[b:b + 1, :] = jnp.transpose(level)[:1, :]
+            part_copy(sl, near_edge).start()
+
+        attend_page(1, far_edge, finish)
+        level_copy(near_edge).start()
         attend_page(0, far_edge)
         for h in range(heads):
             sl = slice(h * fresh, (h + 1) * fresh)
@@ -470,8 +523,6 @@
 
     @pl.when(edge)
     def _():
-        route()
-
         @pl.when(ci > 0)
         def _():
             arrive_fresh(beside_edge)
@@ -481,8 +532,9 @@
             arrive(beside_edge, c)
             split(beside_edge, c)
         attend_page(0, beside_edge)
-        for c in part_copies(ci):
-            c.wait_recv()
+        route()
+        part_copy(slice(0, stacked), ci).wait_recv()
+        level_copy(ci).wait_recv()
         per = block_rows // fresh
         for b in range(stacked // block_rows):
             sl = slice(b * block_rows, (b + 1) * block_rows)
@@ -602,10 +654,15 @@
 
     dispatch(0)
     for n in range(1, ctx_count):
+        if n == 2:
+            pl.when(inner)(lambda: experts(1))
         dispatch(n)
         if n == 1:
             copies_w[2].wait()
-        experts(n - 1)
+        if n == 2:
+            pl.when(edge)(lambda: experts(1))
+        else:
+            experts(n - 1)
         if n > 2:
             mixing(n - 2)
     experts(ctx_count - 1)
@@ -658,8 +715,19 @@
         def _():
             sent(cached, 2)
 
-        for c in part_copies(near_edge):
-            c.wait_send()
+        part_copy(slice(0, stacked), near_edge).wait_send()
+        level_copy(near_edge).wait_send()
+
+
+def settle(context, layer, context_out, layer_out, sem):
+    copies = [
+        pltpu.make_async_copy(context, context_out, sem.at[0]),
+        pltpu.make_async_copy(layer, layer_out, sem.at[1]),
+    ]
+    for c in copies:
+        c.start()
+    for c in copies:
+        c.wait()
 
 
 def fused_device(
@@ -727,6 +795,7 @@
             V((ctx_count, rows, width), BF),
             V((ctx_count, rows, width), BF),
             dma((1,)), dma((6,)), dma((3,)), dma((ctx_count, halves + 1)), dma((3,)), dma((2,)), dma((4,)),
+            pltpu.SemaphoreType.REGULAR((3,)),
             dma((1,)), dma((1,)), dma((1,)), dma((1,)), dma((1,)), dma((pieces,)), dma((1,)), dma((ctx_count,)),
             dma((1,)), dma((ctx_count,)), dma((1,)), dma((ctx_count,)), dma((1,)), dma((ctx_count,)),
         ],
@@ -736,6 +805,19 @@
     )(
         cached_lengths, queries[0], pages[0], residual_in[0], norm_gain.reshape(1, width),
         expert_ids[0].T, route_scores[0].T, out_weight, expert_input[0], expert_output[0],
+    )
+    context, layer_out = pl.pallas_call(
+        settle,
+        out_shape=(
+            jax.ShapeDtypeStruct(context.shape, BF),
+            jax.ShapeDtypeStruct(layer_out.shape, BF),
+        ),
+        in_specs=[vm, vm],
+        out_specs=(hbm, hbm),
+        scratch_shapes=[dma((2,))],
+    )(
+        pltpu.with_memory_space_constraint(context, pltpu.VMEM),
+        pltpu.with_memory_space_constraint(layer_out, pltpu.VMEM),
     )
     return context[None], layer_out[None]
 

time: 53.1 us -> 51.5 us (0.970)
  local copies, waits for them, and re-layouts: 1.29 us -> 0 us
    unnamed x2 -> x0, local copies, waits for them, and re-layouts: 1.29 us -> none
    pallas_call x1, Pallas kernels: 51 us -> 50.1 us  [fused_device(): pl.pallas_call(functools.partial(fused_kernel, ctx_count, exp_count, capa...]
    pallas_call x0 -> x1, Pallas kernels: none -> 0.69 us  [fused_device(): pl.pallas_call(settle, out_shape=(jax.ShapeDtypeStruct(context.shape, BF)...]
where the time goes in v3:
time: 51.5 us; the launch traced here: 51.4 us
  Pallas kernels  50.8 us (99%)
  between operations  0.64 us (1%)
    pallas_call x1, Pallas kernels, fused_device(): pl.pallas_call(functools.partial(fused_kernel, ctx_count, exp_count, capa...  50.1 us

profile of v3, /device:TPU:0, one launch (start us, length us, event | category | flops | bytes accessed | tf_op | source)
XLA Modules:
  0.0 51.4 jit_solution(641773877411872137)
XLA Ops:
  0.6 50.1 %shard_map.113 = (bf16[64,1024]{1,0:T(8,128)(2,1)S(1)}, bf16[16,2048]{1,0:T(8,128)(2,1)S(1)}) custom-call(s32[1,4]{1,0:T(1,128)} %lengths.1, bf16[64,1024]{1,0:T(8,128)(2,1)} %bitcast.17, bf16[576,2,128]{2,1,0:T(2,128)(2,1)} %bitcast.16, bf16[16,2048]{1,0:T(8,128)(2,1)} %bitcast.18, f32[1,2048]{1,0:T(1,128)} %bitcast.19, s32[8,16]{1,0:T(8,128)} %bitcast.20, ...), custom_call_target="tpu_custom_call" | custom-call | tf_op jit(solution)/shard_map/pallas_call | solution.py:754
  50.7 0.7 %shard_map.114 = (bf16[64,1024]{1,0:T(8,128)(2,1)}, bf16[16,2048]{1,0:T(8,128)(2,1)}) custom-call(bf16[64,1024]{1,0:T(8,128)(2,1)S(1)} %get-tuple-element.6.context, bf16[16,2048]{1,0:T(8,128)(2,1)S(1)} %get-tuple-element.7.layer), custom_call_target="tpu_custom_call" | custom-call | tf_op jit(solution)/shard_map/pallas_call | solution.py:809

commit v4 on v3

--- a/solution.py
+++ b/solution.py
@@ -653,18 +653,15 @@
         mix_copy(n).start()
 
     dispatch(0)
-    for n in range(1, ctx_count):
-        if n == 2:
-            pl.when(inner)(lambda: experts(1))
-        dispatch(n)
-        if n == 1:
-            copies_w[2].wait()
-        if n == 2:
-            pl.when(edge)(lambda: experts(1))
-        else:
-            experts(n - 1)
-        if n > 2:
-            mixing(n - 2)
+    dispatch(1)
+    copies_w[2].wait()
+    experts(0)
+    pl.when(inner)(lambda: experts(1))
+    dispatch(2)
+    dispatch(3)
+    pl.when(edge)(lambda: experts(1))
+    experts(2)
+    mixing(1)
     experts(ctx_count - 1)
     for n in range(max(1, ctx_count - 2), ctx_count):
         mixing(n)

time: 51.5 us -> 51.2 us (level)
  no operation moved by 1% of the time
where the time goes in v4:
time: 51.2 us; the launch traced here: 51 us
  Pallas kernels  50.4 us (98%)
  between operations  0.64 us (1%)
    pallas_call x1, Pallas kernels, fused_device(): pl.pallas_call(functools.partial(fused_kernel, ctx_count, exp_count, capa...  49.7 us

profile of v4, /device:TPU:0, one launch (start us, length us, event | category | flops | bytes accessed | tf_op | source)
XLA Modules:
  0.0 51.0 jit_solution(8569275435392628214)
XLA Ops:
  0.6 49.7 %shard_map.113 = (bf16[64,1024]{1,0:T(8,128)(2,1)S(1)}, bf16[16,2048]{1,0:T(8,128)(2,1)S(1)}) custom-call(s32[1,4]{1,0:T(1,128)} %lengths.1, bf16[64,1024]{1,0:T(8,128)(2,1)} %bitcast.17, bf16[576,2,128]{2,1,0:T(2,128)(2,1)} %bitcast.16, bf16[16,2048]{1,0:T(8,128)(2,1)} %bitcast.18, f32[1,2048]{1,0:T(1,128)} %bitcast.19, s32[8,16]{1,0:T(8,128)} %bitcast.20, ...), custom_call_target="tpu_custom_call" | custom-call | tf_op jit(solution)/shard_map/pallas_call | solution.py:751
  50.3 0.7 %shard_map.114 = (bf16[64,1024]{1,0:T(8,128)(2,1)}, bf16[16,2048]{1,0:T(8,128)(2,1)}) custom-call(bf16[64,1024]{1,0:T(8,128)(2,1)S(1)} %get-tuple-element.6.context, bf16[16,2048]{1,0:T(8,128)(2,1)S(1)} %get-tuple-element.7.layer), custom_call_target="tpu_custom_call" | custom-call | tf_op jit(solution)/shard_map/pallas_call | solution.py:806

commit v5 on v4

--- a/solution.py
+++ b/solution.py
@@ -661,9 +661,8 @@
     dispatch(3)
     pl.when(edge)(lambda: experts(1))
     experts(2)
-    mixing(1)
     experts(ctx_count - 1)
-    for n in range(max(1, ctx_count - 2), ctx_count):
+    for n in range(1, ctx_count):
         mixing(n)
     out = hidden[...].astype(F32) + mixing(0)
     for n in range(1, ctx_count):

time: 51.2 us -> 51.5 us (level)
  no operation moved by 1% of the time
where the time goes in v5:
time: 51.5 us; the launch traced here: 51.3 us
  Pallas kernels  50.7 us (98%)
  between operations  0.64 us (1%)
    pallas_call x1, Pallas kernels, fused_device(): pl.pallas_call(functools.partial(fused_kernel, ctx_count, exp_count, capa...  50 us

profile of v5, /device:TPU:0, one launch (start us, length us, event | category | flops | bytes accessed | tf_op | source)
XLA Modules:
  0.0 51.3 jit_solution(17929168163209490890)
XLA Ops:
  0.6 50.0 %shard_map.113 = (bf16[64,1024]{1,0:T(8,128)(2,1)S(1)}, bf16[16,2048]{1,0:T(8,128)(2,1)S(1)}) custom-call(s32[1,4]{1,0:T(1,128)} %lengths.1, bf16[64,1024]{1,0:T(8,128)(2,1)} %bitcast.17, bf16[576,2,128]{2,1,0:T(2,128)(2,1)} %bitcast.16, bf16[16,2048]{1,0:T(8,128)(2,1)} %bitcast.18, f32[1,2048]{1,0:T(1,128)} %bitcast.19, s32[8,16]{1,0:T(8,128)} %bitcast.20, ...), custom_call_target="tpu_custom_call" | custom-call | tf_op jit(solution)/shard_map/pallas_call | solution.py:750
  50.6 0.7 %shard_map.114 = (bf16[64,1024]{1,0:T(8,128)(2,1)}, bf16[16,2048]{1,0:T(8,128)(2,1)}) custom-call(bf16[64,1024]{1,0:T(8,128)(2,1)S(1)} %get-tuple-element.6.context, bf16[16,2048]{1,0:T(8,128)(2,1)S(1)} %get-tuple-element.7.layer), custom_call_target="tpu_custom_call" | custom-call | tf_op jit(solution)/shard_map/pallas_call | solution.py:805
